TPU v7x, 32 devices: a whole 2x2x4 slice. The times are simulated.
32 devices in a mesh: elem: 16 (over z, x, core), section: 2 (over y).
Axes of the slice: x: 2, y: 2, z: 4, core: 2. Of those that a mesh axis runs over, the one named last changes fastest.
Arguments:
- u_start: float32 [512, 320], P('elem'), may hold values from -6 to 6
- inverses: float32 [512, 320, 320], P('elem'), may hold values from -1 to 2
- neighbours: int32 [512, 5], P('elem'), may hold values from 0 to 511, as said below
- partners: int32 [512], replicated, may hold values from 0 to 511, as said below
Outputs:
- section_states: float32 [4, 512, 320], P('section', 'elem')
Inputs may be any that keep to these rules, and one draw needn't show every extreme that they name: `neighbours`: every entry names an element on the same device as the row's element, or on the device just before or after it along elem, cyclically. The partners of the 32 elements of device d along elem lie on devices d + 4 and d + 5, cyclically, 16 on each.
All inputs are finite; a program needn't handle non-finite values.
Results may differ from a plain program's by a relative error of at most 0.0001.
Values sent between devices are 32-bit elements; how exact they have to be, the bound alone decides.
A program may use at most 64 MiB of HBM per device.

v0:
```python
import functools
import math

import jax
import jax.numpy as jnp
from jax import lax
from jax.experimental import pallas as pl
from jax.experimental.pallas import tpu as pltpu
from jax.sharding import PartitionSpec as P

NODE1 = 4
SECTIONS = 4
NEWTON = 2


time_step = 0.03
dissipation = 2.0
enthalpy_factor = 3.5
radau_nodes = [0.08858795951270394, 0.4094668644407347, 0.787659461760847, 1.0]


def lobatto():
    node_count = NODE1
    inner_value = 1.0 / math.sqrt(5.0)
    lobatto_nodes = [-1.0, -inner_value, inner_value, 1.0]
    products = []
    for row in range(node_count):
        value = 1.0
        for other in range(node_count):
            if other != row:
                value = value * (lobatto_nodes[row] - lobatto_nodes[other])
        products.append(value)
    derivative = []
    for row in range(node_count):
        entries = []
        for column in range(node_count):
            if row == column:
                total = 0.0
                for other in range(node_count):
                    if other != row:
                        total = total + 1.0 / (lobatto_nodes[row] - lobatto_nodes[other])
                entries.append(2.0 * total)
            else:
                entries.append(
                    2.0
                    * (products[row] / products[column])
                    / (lobatto_nodes[row] - lobatto_nodes[column])
                )
        derivative.append(entries)
    return derivative, float(node_count * (node_count - 1) / 2.0)


def radau_table():
    section_total = SECTIONS
    butcher = []
    columns = []
    for column in range(section_total):
        coeffs = [1.0]
        scale = 1.0
        for other in range(section_total):
            if other != column:
                shifted = [0.0] + coeffs
                for position in range(len(coeffs)):
                    shifted[position] = shifted[position] - radau_nodes[other] * coeffs[position]
                coeffs = shifted
                scale = scale * (radau_nodes[column] - radau_nodes[other])
        integral = [0.0] + [
            coeffs[position] / (position + 1.0) / scale for position in range(len(coeffs))
        ]
        columns.append(integral)
    for row in range(section_total):
        entries = []
        for column in range(section_total):
            value = 0.0
            for coefficient in reversed(columns[column]):
                value = value * radau_nodes[row] + coefficient
            entries.append(value)
        butcher.append(entries)
    return butcher


FIELDS = 5
NODES = NODE1**3
FACE = NODE1**2
LANES = 128
GROUP = 8
ROWS = 64
MATRIX = 3
MESH = pl.DeviceIdType.MESH


def strided(start, count):
    return pl.ds(start, count, stride=NODE1)


def to_k_order(src_ref, k_ref):
    for field in range(FIELDS):
        for k in range(NODE1):
            base = field * NODES
            k_ref[base + k * FACE : base + (k + 1) * FACE, :] = src_ref[strided(base + k, FACE), :]


def slab(src_ref, k_ref, direction, position):
    out = []
    for field in range(FIELDS):
        base = field * NODES
        if direction == 0:
            out.append(src_ref[base + position * FACE : base + (position + 1) * FACE, :])
        elif direction == 1:
            out.append(k_ref[strided(base + position, FACE), :])
        else:
            out.append(k_ref[base + position * FACE : base + (position + 1) * FACE, :])
    return out


def put_slabs(out_ref, k_ref, direction, slabs):
    for position in range(NODE1):
        for field in range(FIELDS):
            base = field * NODES
            rows = slice(base + position * FACE, base + (position + 1) * FACE)
            value = slabs[position][field]
            if direction == 0:
                out_ref[rows, :] = value
            elif direction == 1:
                k_ref[strided(base + position, FACE), :] = value
            else:
                value = k_ref[rows, :] + value
                there = strided(base + position, FACE)
                out_ref[there, :] = out_ref[there, :] + value


def speed2(state):
    return state[1] * state[1] + state[2] * state[2] + state[3] * state[3]


def two_point(a, ka, b, kb, direction):
    r = a[0] + b[0]
    v = [a[1 + c] + b[1 + c] for c in range(3)]
    p = a[4] + b[4]
    n = v[direction]
    m = (0.25 * r) * n
    half = 0.5 * m
    out = [m]
    for c in range(3):
        term = half * v[c]
        if c == direction:
            term = term + 0.5 * p
        out.append(term)
    out.append((0.25 * enthalpy_factor * p) * n + (0.5 * half) * (ka + kb))
    return out


def volume(uc, uk, out_ref, tk, scale):
    deriv, _ = lobatto()
    for direction in range(3):
        states = [slab(uc, uk, direction, pos) for pos in range(NODE1)]
        speeds = [speed2(state) for state in states]
        sums = [None] * NODE1
        for a in range(NODE1):
            for b in range(a + 1, NODE1):
                f = two_point(states[a], speeds[a], states[b], speeds[b], direction)
                for at, other in ((a, b), (b, a)):
                    c = -2.0 * scale * deriv[at][other]
                    terms = [c * x for x in f]
                    sums[at] = terms if sums[at] is None else [x + y for x, y in zip(sums[at], terms)]
        put_slabs(out_ref, tk, direction, sums)


def surface(uc, uk, faces, out_ref, tk, scale):
    _, inv_weight = lobatto()

    def terms(face):
        direction, upper = face // 2, face % 2
        own = slab(uc, uk, direction, (NODE1 - 1) * upper)
        other = faces(face)
        f = two_point(own, speed2(own), other, speed2(other), direction)
        c = -2.0 * scale * inv_weight
        d = 0.5 * dissipation * c
        sign = 2.0 * upper - 1.0
        return [(c * sign) * x - d * (n - u) for x, n, u in zip(f, other, own)]

    add_faces(terms, out_ref, tk)


def add_faces(terms, out_ref, tk):
    zero = jnp.zeros((FACE, LANES), jnp.float32)
    for face in range(6):
        direction, position = face // 2, (NODE1 - 1) * (face % 2)
        values = terms(face)
        for field in range(FIELDS):
            base = field * NODES
            rows = slice(base + position * FACE, base + (position + 1) * FACE)
            there = strided(base + position, FACE)
            if direction == 0:
                out_ref[rows, :] = out_ref[rows, :] + values[field]
            elif direction == 1:
                tk[there, :] = values[field]
                if face == 3:
                    for inner in range(1, NODE1 - 1):
                        tk[strided(base + inner, FACE), :] = zero
            else:
                tk[rows, :] = tk[rows, :] + values[field]
    for field in range(FIELDS):
        base = field * NODES
        for position in range(NODE1):
            rows = slice(base + position * FACE, base + (position + 1) * FACE)
            there = strided(base + position, FACE)
            out_ref[there, :] = out_ref[there, :] + tk[rows, :]


def lift(faces, out_ref, tk):
    zero = jnp.zeros((FACE, LANES), jnp.float32)
    for direction in range(3):
        slabs = [[zero] * FIELDS for _ in range(NODE1)]
        slabs[0] = faces(2 * direction)
        slabs[NODE1 - 1] = faces(2 * direction + 1)
        put_slabs(out_ref, tk, direction, slabs)


def kernel(
    devices, count, u_in, nbr_in, partner_in, inv_ref, out_ref,
    u_ref, nbr_ref, partner_ref,
    a_ref, recv_ref, zrecv_ref, zsend_ref, pick_ref, near_ref,
    uc, uk, vc, wc, lc, tk, nc, nk, fc, gc, all_rows, low_rows, half_ref, w_ref, dot_ref, xr,
    in_sem, a_sem, send_sem, recv_sem,
):
    rank = lax.axis_index("elem")
    part = lax.axis_index("section")
    parts = lax.axis_size("section")
    own_sections = SECTIONS // parts
    rotation = devices // 4
    unknowns = FIELDS * NODES
    butcher = radau_table()
    _, inv_weight = lobatto()
    groups = count // GROUP

    def at(offset):
        return lax.rem(rank + (offset + devices), devices)

    def load(g):
        block = pl.ds(g * GROUP, GROUP)
        return pltpu.make_async_copy(inv_ref.at[block], a_ref.at[block], a_sem.at[g])

    barrier = pltpu.get_barrier_semaphore()
    others = (1, -1, rotation, -rotation, rotation + 1, -rotation - 1)
    for offset in others:
        pl.semaphore_signal(barrier, inc=1, device_id={"elem": at(offset)}, device_id_type=MESH)
    small = [
        pltpu.make_async_copy(src, dst, in_sem.at[index])
        for index, (src, dst) in enumerate(
            ((u_in, u_ref), (nbr_in, nbr_ref), (partner_in, partner_ref))
        )
    ]
    for each in small:
        each.start()
    for g in range(groups):
        load(g).start()

    def copy(x, which, start=0, size=count):
        if which < 2:
            src = u_ref if x == 0 else recv_ref.at[x, pl.ds(2 * count + start, size)]
            dst = recv_ref.at[x, pl.ds(which * count + start, size)]
            target = at(1) if which == 0 else at(-1)
        else:
            src = zsend_ref.at[x, pl.ds(start, size)]
            dst = zrecv_ref.at[x, pl.ds((which - 2) * count + start, size)]
            target = at(-rotation) if which == 2 else at(-rotation - 1)
        return pltpu.make_async_remote_copy(
            src_ref=src, dst_ref=dst, send_sem=send_sem.at[x, which],
            recv_sem=recv_sem.at[x, which], device_id={"elem": target}, device_id_type=MESH,
        )

    def lower_rows(col_ref):
        low = col_ref[strided(0, FIELDS * FACE), :]
        low = jnp.concatenate([low, jnp.zeros((LANES - FIELDS * FACE, LANES), jnp.float32)], axis=0)
        return low.T

    def send(x, vectors, g, dst):
        start = pl.multiple_of(g * GROUP, GROUP)
        low_rows[...] = lower_rows(dst)
        all_rows[...] = dst[...].T
        for v in range(vectors):
            zsend_ref[x + v, pl.ds(start, GROUP)] = low_rows[pl.ds(v * count + start, GROUP), :]
        for v in range(vectors):
            copy(x + v, 3, start, GROUP).start()
            copy(x + v, 2, start, GROUP).start()
        for v in range(vectors):
            recv_ref[x + v, pl.ds(2 * count + start, GROUP)] = all_rows[pl.ds(v * count + start, GROUP), :]
        for v in range(vectors):
            copy(x + v, 0, start, GROUP).start()
            copy(x + v, 1, start, GROUP).start()

    for each in small:
        each.wait()
    u_rows = u_ref[...]
    uc[...] = jnp.concatenate([u_rows] * SECTIONS, axis=0).T
    zsend_ref[0] = lower_rows(uc)[:count]
    recv_ref[0, 2 * count : 3 * count] = u_rows
    pl.semaphore_wait(barrier, len(others))
    copy(0, 3).start()
    copy(0, 2).start()
    copy(0, 0).start()
    copy(0, 1).start()
    to_k_order(uc, uk)
    volume(uc, uk, lc, tk, 1.0)

    lane = lax.broadcasted_iota(jnp.int32, (1, LANES), 1)
    block = lane // count
    local = lane - block * count
    row = lax.broadcasted_iota(jnp.int32, (LANES, 1), 0)

    def ids(*offsets):
        out = jnp.full((LANES, 1), -1, jnp.int32)
        for index, offset in enumerate(offsets):
            inside = (row >= index * count) & (row < (index + 1) * count)
            out = jnp.where(inside, at(offset) * count + row - index * count, out)
        return out

    side_ids = ids(-1, 1, 0)
    sliding_ids = ids(rotation, rotation + 1)
    per_row = LANES // count
    listed = partner_ref[pl.ds(rank // per_row, 1), :]
    partner = jnp.zeros((1, LANES), jnp.int32)
    for index in range(per_row):
        part_row = jnp.concatenate([listed[:, index * count : (index + 1) * count]] * SECTIONS, axis=1)
        partner = jnp.where(rank % per_row == index, part_row, partner)
    for face in range(6):
        if face < 5:
            wanted = jnp.concatenate([nbr_ref[face : face + 1, :]] * SECTIONS, axis=1)
            match = side_ids == wanted
        else:
            match = sliding_ids == partner
        pick_ref[face] = jnp.where(match, 1.0, 0.0).astype(jnp.bfloat16)

    def picked(face, values):
        high = values.astype(jnp.bfloat16)
        rest = values - high.astype(jnp.float32)
        middle = rest.astype(jnp.bfloat16)
        low = (rest - middle.astype(jnp.float32)).astype(jnp.bfloat16)
        split = jnp.concatenate([high, middle, low], axis=0)
        got = lax.dot_general(
            split, pick_ref[face], (((1,), (0,)), ((), ())), preferred_element_type=jnp.float32
        )
        n = values.shape[0]
        return (got[2 * n :] + got[n : 2 * n]) + got[:n]

    def receive(x, put):
        for which in range(4):
            copy(x, which).wait_recv()
        mine = recv_ref[x]
        nc[...] = jnp.concatenate([mine, mine[2 * count :]], axis=0).T
        to_k_order(nc, nk)
        for face in range(5):
            position = (NODE1 - 1) * (1 - face % 2)
            put(face, picked(face, jnp.concatenate(slab(nc, nk, face // 2, position), axis=0)))
        sliding = zrecv_ref[x]
        sliding = jnp.concatenate([sliding, sliding], axis=0).T
        put(5, picked(5, sliding[: FIELDS * FACE]))

    def keep(slot):
        def put(face, value):
            near_ref[slot, face] = value
        return put

    def near(slot):
        def faces(face):
            return [near_ref[slot, face, f * FACE : (f + 1) * FACE, :] for f in range(FIELDS)]
        return faces

    def per_lane(value_of):
        out = jnp.zeros((1, LANES), jnp.float32)
        for group in range(SECTIONS):
            value = jnp.float32(value_of(0, group))
            for other in range(1, parts):
                value = jnp.where(part == other, jnp.float32(value_of(other, group)), value)
            out = jnp.where(block == group, value, out)
        return out

    cycle = lane % GROUP
    eighth = lane // GROUP

    def stacked(high, low, axis):
        cut = 2 * LANES
        parts_of = [lax.slice_in_dim(t, 0, cut, axis=axis) for t in (high, low)]
        parts_of += [lax.slice_in_dim(t, cut, unknowns, axis=axis) for t in (high, low)]
        return jnp.concatenate(parts_of, axis=axis)

    def halves():
        @pl.loop(0, groups)
        def _(g):
            load(g).wait()
            for k in range(MATRIX):
                for c in range(unknowns // ROWS):
                    a = a_ref[g * GROUP + GROUP - MATRIX + k, c * ROWS : (c + 1) * ROWS, :]
                    high = a.astype(jnp.bfloat16).astype(jnp.float32)
                    to = k * unknowns + c * ROWS
                    both = stacked(high, a - high, 1)
                    half_ref[g, to : to + ROWS, :] = both.astype(jnp.bfloat16)

    def operand(value):
        xr[...] = value.T
        high = value.astype(jnp.bfloat16).astype(jnp.float32)
        low = pltpu.roll(value - high, LANES // 2, 1)
        both = jnp.where(lane < LANES // 2, high, low)
        w_ref[...] = stacked(both, both, 0).astype(jnp.bfloat16)

    def matvec(dst, vectors, x=None):
        dst[...] = jnp.zeros_like(dst)
        vector_part = GROUP - MATRIX if vectors == 2 else GROUP

        @pl.loop(0, groups)
        def _(g):
            if vectors == 2:
                dot_ref[...] = jnp.dot(
                    half_ref[g], w_ref[...], preferred_element_type=jnp.float32
                )
            xs = [
                xr[pl.ds(pl.multiple_of(v * count + g * GROUP, GROUP), GROUP), :]
                for v in range(vectors)
            ]
            for c in range(unknowns // ROWS):
                rows = slice(c * ROWS, (c + 1) * ROWS)
                accs = [jnp.zeros((ROWS, LANES), jnp.float32)] * vectors
                for k in range(vector_part):
                    a = a_ref[g * GROUP + k, rows, :]
                    for v in range(vectors):
                        total = jnp.sum(a * xs[v][k : k + 1, :], axis=1, keepdims=True)
                        accs[v] = jnp.where(cycle == k, total, accs[v])
                full = dst[rows, :]
                for v in range(vectors):
                    if vectors == 1:
                        here = local // GROUP == g
                    else:
                        here = eighth == v * groups + g
                    full = jnp.where(here & (cycle < vector_part), accs[v], full)
                dst[rows, :] = full
            if vectors == 2:
                for c in range(unknowns // ROWS):
                    rows = slice(c * ROWS, (c + 1) * ROWS)
                    got = dot_ref[rows, :]
                    for k in range(1, MATRIX):
                        more = dot_ref[k * unknowns + c * ROWS : k * unknowns + (c + 1) * ROWS, :]
                        got = jnp.where(cycle == vector_part + k, more, got)
                    got = got + pltpu.roll(got, LANES // 2, 1)
                    here = (block < 2) & (local // GROUP == g) & (cycle >= vector_part)
                    dst[rows, :] = jnp.where(here, got, dst[rows, :])
            if x is not None:
                send(x, vectors, g, dst)

    halves()

    receive(0, keep(0))
    surface(uc, uk, near(0), lc, tk, 1.0)
    xr[...] = lc[...].T
    matvec(vc, 1, 1)
    receive(1, keep(1))
    lift(near(1), lc, tk)
    xr[...] = lc[...].T
    matvec(wc, 1, 2)

    def alpha(i):
        return time_step * sum(butcher[i])

    def coupling(i):
        return time_step * butcher[i][i] * dissipation * inv_weight

    def own(p, group):
        return p * own_sections + group % own_sections

    alphas = per_lane(lambda p, s: alpha(s))
    betas = per_lane(lambda p, s: alpha(s) * coupling(s))
    gc[...] = uc[...] + alphas * vc[...] + betas * wc[...]
    to_k_order(gc, uk)

    def add(face, value):
        near_ref[0, face] = near_ref[0, face] + alphas * near_ref[1, face] + betas * value

    volume(gc, uk, lc, tk, time_step)
    receive(2, add)
    surface(gc, uk, near(0), lc, tk, time_step)

    own_alphas = per_lane(lambda p, g: alpha(own(p, g)))
    own_betas = per_lane(lambda p, g: alpha(own(p, g)) * coupling(own(p, g)))
    own_couplings = per_lane(lambda p, g: coupling(own(p, g)))
    step = own_alphas * vc[...] + own_betas * wc[...]
    tend = lc[...]
    total = -step
    for shift in range(SECTIONS):
        moved = tend if shift == 0 else pltpu.roll(tend, shift * count, 1)
        weights = per_lane(lambda p, g: butcher[own(p, g)][(g - shift) % SECTIONS])
        total = total + weights * moved
    gc[...] = step
    operand(total)
    matvec(fc, own_sections, 3)
    receive(3, keep(0))
    for s in range(1, own_sections):
        def merge(face, value, s=s):
            near_ref[0, face] = jnp.where(block == s, value, near_ref[0, face])
        receive(3 + s, merge)
    lift(near(0), lc, tk)
    operand(own_couplings * lc[...])
    matvec(wc, own_sections)
    rows = (gc[...] + fc[...] + wc[...]).T
    for s in range(own_sections):
        out_ref[s] = rows[s * count : (s + 1) * count]
    for x in range(3 + own_sections):
        for which in range(4):
            copy(x, which).wait_send()


def on_device(u_start, inverses, neighbours, partners):
    count, unknowns = u_start.shape
    devices = lax.axis_size("elem")
    own_sections = SECTIONS // lax.axis_size("section")
    listed = partners.reshape(-1, LANES)
    exchanges = 3 + own_sections
    column = pltpu.VMEM((unknowns, LANES), jnp.float32)
    vmem = pl.BlockSpec(memory_space=pltpu.VMEM)
    change = pl.pallas_call(
        functools.partial(kernel, devices, count),
        out_shape=jax.ShapeDtypeStruct((own_sections, count, unknowns), jnp.float32),
        in_specs=[pl.BlockSpec(memory_space=pl.ANY)] * 4,
        out_specs=vmem,
        scratch_shapes=[
            pltpu.VMEM(u_start.shape, jnp.float32),
            pltpu.VMEM(neighbours.shape[::-1], jnp.int32),
            pltpu.VMEM(listed.shape, jnp.int32),
            pltpu.VMEM((count, unknowns, unknowns), jnp.float32),
            pltpu.VMEM((exchanges, 3 * count, unknowns), jnp.float32),
            pltpu.VMEM((exchanges, 2 * count, LANES), jnp.float32),
            pltpu.VMEM((exchanges, count, LANES), jnp.float32),
            pltpu.VMEM((6, LANES, LANES), jnp.bfloat16),
            pltpu.VMEM((2, 6, FIELDS * FACE, LANES), jnp.float32),
        ]
        + [column] * 10
        + [
            pltpu.VMEM((LANES, unknowns), jnp.float32),
            pltpu.VMEM((LANES, LANES), jnp.float32),
            pltpu.VMEM((count // GROUP, MATRIX * unknowns, 2 * unknowns), jnp.bfloat16),
            pltpu.VMEM((2 * unknowns, LANES), jnp.bfloat16),
            pltpu.VMEM((MATRIX * unknowns, LANES), jnp.float32),
            pltpu.VMEM((LANES, unknowns), jnp.float32),
            pltpu.SemaphoreType.DMA((3,)),
            pltpu.SemaphoreType.DMA((count // GROUP,)),
            pltpu.SemaphoreType.DMA((exchanges, 4)),
            pltpu.SemaphoreType.DMA((exchanges, 4)),
        ],
        compiler_params=pltpu.CompilerParams(
            collective_id=0, has_side_effects=True, vmem_limit_bytes=67_043_328
        ),
    )(u_start, neighbours.T, listed, inverses)
    return u_start[None] + change


def solution(mesh):
    placed = (P("elem", None), P("elem", None, None), P("elem", None), P())
    return jax.shard_map(
        on_device, mesh=mesh, in_specs=placed, out_specs=P("section", "elem", None), check_vma=False
    )
```

profile of v0, /device:TPU:0, one launch (start us, length us, event | category | flops | bytes accessed | tf_op | source)
XLA Modules:
  0.0 37.8 jit_solution(12278087827054668812)
XLA Ops:
  0.0 36.3 %shard_map.46 = f32[2,32,320]{2,1,0:T(8,128)} custom-call(f32[32,320]{1,0:T(8,128)} %u_in.1, s32[5,32]{1,0:T(8,128)} %bitcast.2, s32[4,128]{1,0:T(4,128)} %bitcast.3, f32[32,320,320]{2,1,0:T(8,128)} %inv_ref.1), custom_call_target="tpu_custom_call" | custom-call | tf_op jit(solution)/shard_map/pallas_call | solution.py:519
  36.3 1.5 %broadcast_add_fusion = f32[2,32,320]{2,1,0:T(8,128)} fusion(f32[2,32,320]{2,1,0:T(8,128)} %shard_map.46, f32[32,320]{1,0:T(8,128)} %u_in.1), kind=kLoop, calls=%fused_computation | loop fusion | flops 20480 | bytes 204800 | tf_op jit(solution)/shard_map/add | solution.py:552
where the time goes:
time: 38 us; the launch traced here: 37.8 us
  Pallas kernels  36.3 us (96%)
  other arithmetic  1.55 us (4%)
    pallas_call x1, Pallas kernels, on_device(): pl.pallas_call(functools.partial(kernel, devices, count), out_shape=jax.S...  36.3 us
    add x1, other arithmetic, on_device(): return u_start[None] + change  1.55 us

commit v1 on v0

v1 whole, which is shorter than its diff:
```python
import functools
import math

import jax
import jax.numpy as jnp
from jax import lax
from jax.experimental import pallas as pl
from jax.experimental.pallas import tpu as pltpu
from jax.sharding import PartitionSpec as P

NODE1 = 4
SECTIONS = 4
NEWTON = 2


time_step = 0.03
dissipation = 2.0
enthalpy_factor = 3.5
radau_nodes = [0.08858795951270394, 0.4094668644407347, 0.787659461760847, 1.0]


def lobatto():
    node_count = NODE1
    inner_value = 1.0 / math.sqrt(5.0)
    lobatto_nodes = [-1.0, -inner_value, inner_value, 1.0]
    products = []
    for row in range(node_count):
        value = 1.0
        for other in range(node_count):
            if other != row:
                value = value * (lobatto_nodes[row] - lobatto_nodes[other])
        products.append(value)
    derivative = []
    for row in range(node_count):
        entries = []
        for column in range(node_count):
            if row == column:
                total = 0.0
                for other in range(node_count):
                    if other != row:
                        total = total + 1.0 / (lobatto_nodes[row] - lobatto_nodes[other])
                entries.append(2.0 * total)
            else:
                entries.append(
                    2.0
                    * (products[row] / products[column])
                    / (lobatto_nodes[row] - lobatto_nodes[column])
                )
        derivative.append(entries)
    return derivative, float(node_count * (node_count - 1) / 2.0)


def radau_table():
    section_total = SECTIONS
    butcher = []
    columns = []
    for column in range(section_total):
        coeffs = [1.0]
        scale = 1.0
        for other in range(section_total):
            if other != column:
                shifted = [0.0] + coeffs
                for position in range(len(coeffs)):
                    shifted[position] = shifted[position] - radau_nodes[other] * coeffs[position]
                coeffs = shifted
                scale = scale * (radau_nodes[column] - radau_nodes[other])
        integral = [0.0] + [
            coeffs[position] / (position + 1.0) / scale for position in range(len(coeffs))
        ]
        columns.append(integral)
    for row in range(section_total):
        entries = []
        for column in range(section_total):
            value = 0.0
            for coefficient in reversed(columns[column]):
                value = value * radau_nodes[row] + coefficient
            entries.append(value)
        butcher.append(entries)
    return butcher


FIELDS = 5
NODES = NODE1**3
FACE = NODE1**2
LANES = 128
SUB = 8
CHUNKS = ((0, 2), (2, 2), (4, 1))
LOADS = ((0, 1), (1, 2), (3, 2))
X_SLOT, Y_SLOT, Z_SLOT = 0, 4, 8
VMEM_BYTES = 54 * 2**20
MESH = pl.DeviceIdType.MESH


def strided(start, count):
    return pl.ds(start, count, stride=NODE1)


def to_k_order(src_ref, k_ref):
    for field in range(FIELDS):
        for k in range(NODE1):
            base = field * NODES
            k_ref[base + k * FACE : base + (k + 1) * FACE, :] = src_ref[strided(base + k, FACE), :]


def slab(src_ref, k_ref, direction, position):
    out = []
    for field in range(FIELDS):
        base = field * NODES
        if direction == 0:
            out.append(src_ref[base + position * FACE : base + (position + 1) * FACE, :])
        elif direction == 1:
            out.append(k_ref[strided(base + position, FACE), :])
        else:
            out.append(k_ref[base + position * FACE : base + (position + 1) * FACE, :])
    return out


def put_slabs(out_ref, k_ref, direction, slabs):
    for position in range(NODE1):
        for field in range(FIELDS):
            base = field * NODES
            rows = slice(base + position * FACE, base + (position + 1) * FACE)
            value = slabs[position][field]
            if direction == 0:
                out_ref[rows, :] = value
            elif direction == 1:
                k_ref[strided(base + position, FACE), :] = value
            else:
                value = k_ref[rows, :] + value
                there = strided(base + position, FACE)
                out_ref[there, :] = out_ref[there, :] + value


def speed2(state):
    return state[1] * state[1] + state[2] * state[2] + state[3] * state[3]


def two_point(a, ka, b, kb, direction):
    r = a[0] + b[0]
    v = [a[1 + c] + b[1 + c] for c in range(3)]
    p = a[4] + b[4]
    n = v[direction]
    m = (0.25 * r) * n
    half = 0.5 * m
    out = [m]
    for c in range(3):
        term = half * v[c]
        if c == direction:
            term = term + 0.5 * p
        out.append(term)
    out.append((0.25 * enthalpy_factor * p) * n + (0.5 * half) * (ka + kb))
    return out


def volume(uc, uk, out_ref, tk, scale):
    deriv, _ = lobatto()
    for direction in range(3):
        states = [slab(uc, uk, direction, pos) for pos in range(NODE1)]
        speeds = [speed2(state) for state in states]
        sums = [None] * NODE1
        for a in range(NODE1):
            for b in range(a + 1, NODE1):
                f = two_point(states[a], speeds[a], states[b], speeds[b], direction)
                for at, other in ((a, b), (b, a)):
                    c = -2.0 * scale * deriv[at][other]
                    terms = [c * x for x in f]
                    sums[at] = terms if sums[at] is None else [x + y for x, y in zip(sums[at], terms)]
        put_slabs(out_ref, tk, direction, sums)


def face_terms(own, other, direction, flux_scale, jump_scale):
    f = two_point(own, speed2(own), other, speed2(other), direction)
    return [flux_scale * x - jump_scale * (n - u) for x, n, u in zip(f, other, own)]


def surface(g, near_ref, out_ref, scale):
    _, inv_weight = lobatto()
    c = -2.0 * scale * inv_weight
    d = 0.5 * dissipation * c
    row = lax.broadcasted_iota(jnp.int32, (SUB, LANES), 0)
    top = row < NODE1
    k = row % NODE1
    y_scale = jnp.where(top, -c, c)
    z_scale = jnp.where(k == 0, -c, jnp.where(k == NODE1 - 1, c, 0.0))
    z_jump = jnp.where((k == 0) | (k == NODE1 - 1), d, 0.0)

    for i in range(NODE1):
        rows = [[g_rows(f, i, half) for f in range(FIELDS)] for half in range(2)]
        own = [[g[rows[half][f], :] for f in range(FIELDS)] for half in range(2)]
        total = [
            face_terms(own[half], near_state(near_ref, Z_SLOT + 2 * i + half), 2, z_scale, z_jump)
            for half in range(2)
        ]
        y_own = [jnp.where(top, low, high) for low, high in zip(*own)]
        y_terms = face_terms(y_own, near_state(near_ref, Y_SLOT + i), 1, y_scale, d)
        total = [
            [t + jnp.where(top if half == 0 else ~top, y, 0.0) for t, y in zip(total[half], y_terms)]
            for half in range(2)
        ]
        if i in (0, NODE1 - 1):
            side = 0 if i == 0 else 1
            for half in range(2):
                x_terms = face_terms(
                    own[half], near_state(near_ref, X_SLOT + 2 * side + half), 0, (2 * side - 1) * c, d
                )
                total[half] = [t + x for t, x in zip(total[half], x_terms)]
        for half in range(2):
            for f in range(FIELDS):
                out_ref[rows[half][f], :] = out_ref[rows[half][f], :] + total[half][f]


def g_rows(f, i, half):
    start = f * NODES + i * FACE + half * SUB
    return slice(start, start + SUB)


def c_rows(f, half):
    start = f * FACE + half * SUB
    return slice(start, start + SUB)


def near_state(near_ref, slot):
    return [near_ref[slot, f] for f in range(FIELDS)]


def take(value, index):
    return jnp.take_along_axis(value, index, axis=1, mode="promise_in_bounds")


def kernel(
    devices, count, u_in, nbr_in, partner_in, inv_ref, out_ref,
    u_ref, nbr_ref, partner_ref,
    raw_ref, tt_ref, y_ref, zsend_ref, recv_ref, zrecv_ref, index_ref, near_v, near_ref,
    uc, uk, vc, wc, lc, tk, gc, x_ref, acc_ref, last_ref,
    in_sem, a_sem, send_sem, recv_sem,
):
    rank = lax.axis_index("elem")
    part = lax.axis_index("section")
    parts = lax.axis_size("section")
    own_sections = SECTIONS // parts
    rotation = devices // 4
    unknowns = FIELDS * NODES
    butcher = radau_table()
    _, inv_weight = lobatto()

    def at(offset):
        return lax.rem(rank + (offset + devices), devices)

    barrier = pltpu.get_barrier_semaphore()
    others = (1, -1, rotation, -rotation, rotation + 1, -rotation - 1)
    for offset in others:
        pl.semaphore_signal(barrier, inc=1, device_id={"elem": at(offset)}, device_id_type=MESH)
    small = [
        pltpu.make_async_copy(src, dst, in_sem.at[index])
        for index, (src, dst) in enumerate(
            ((u_in, u_ref), (nbr_in, nbr_ref), (partner_in, partner_ref))
        )
    ]
    for each in small:
        each.start()

    def load(part_of):
        first, fields = LOADS[part_of]
        rows = pl.ds(first * NODES, fields * NODES)
        for e in range(count):
            pltpu.make_async_copy(inv_ref.at[e, rows], raw_ref.at[rows, e], a_sem.at[part_of]).start()

    def loaded(part_of):
        first, fields = LOADS[part_of]
        there = raw_ref.at[pl.ds(first * NODES, fields * NODES)]
        pltpu.make_async_copy(there, there, a_sem.at[part_of]).wait()

    def transposed(f, r):
        for q in range(0, unknowns, LANES):
            width = min(LANES, unknowns - q)
            blocks = [raw_ref[f * NODES + b * FACE + r, :, q : q + width] for b in range(NODE1)]
            tt_ref[f * FACE + r, q : q + width, :] = jnp.concatenate(blocks, axis=0).T

    load(0)

    row = lax.broadcasted_iota(jnp.int32, (SUB, LANES), 0)
    lane = lax.broadcasted_iota(jnp.int32, (SUB, LANES), 1)
    group = lane // count
    local = lane - group * count
    top = row < NODE1
    k_of = row % NODE1
    block = group[:1]

    def copies(x, chunk):
        first, fields = CHUNKS[chunk]
        rows = pl.ds(first * FACE, fields * FACE)
        zrows = pl.ds(chunk * SUB, SUB)
        out = []
        for which in range(4):
            if which < 2:
                src, dst = y_ref.at[x, rows], recv_ref.at[x, which, rows]
                target = at(1) if which == 0 else at(-1)
            else:
                src, dst = zsend_ref.at[x, zrows], zrecv_ref.at[x, which - 2, zrows]
                target = at(-rotation) if which == 2 else at(-rotation - 1)
            slot = chunk * 4 + which
            out.append(pltpu.make_async_remote_copy(
                src_ref=src, dst_ref=dst, send_sem=send_sem.at[x, slot],
                recv_sem=recv_sem.at[x, slot], device_id={"elem": target}, device_id_type=MESH,
            ))
        return out

    def pack(x, chunk):
        first, fields = CHUNKS[chunk]
        packed = jnp.zeros((SUB, LANES), jnp.float32)
        for slot in range(2 * fields):
            value = y_ref[x, c_rows(first + slot // 2, slot % 2), :]
            value = value if slot == 0 else pltpu.roll(value, slot, 0)
            packed = jnp.where(k_of == slot, value, packed)
        zsend_ref[x, chunk * SUB : (chunk + 1) * SUB, :] = packed

    def send(x, chunk):
        pack(x, chunk)
        out = copies(x, chunk)
        for which in (3, 2, 0, 1):
            out[which].start()

    for each in small:
        each.wait()
    uc[...] = jnp.concatenate([u_ref[...]] * SECTIONS, axis=0).T
    for f in range(FIELDS):
        for half in range(2):
            value = uc[g_rows(f, NODE1 - 1, half), :]
            for i in range(NODE1 - 2, -1, -1):
                value = jnp.where(group == i, uc[g_rows(f, i, half), :], value)
            y_ref[0, c_rows(f, half), :] = value

    load(1)
    load(2)

    def found(wanted, offsets):
        index = wanted - at(offsets[0]) * count
        code = jnp.zeros_like(wanted)
        for at_code, offset in enumerate(offsets[1:]):
            here = wanted - at(offset) * count
            match = (here >= 0) & (here < count)
            index = jnp.where(match, here, index)
            code = jnp.where(match, at_code + 1, code)
        return index, code

    def beside(face):
        wanted = jnp.concatenate([nbr_ref[face : face + 1, :]] * SECTIONS, axis=1)
        return found(jnp.broadcast_to(wanted, (SUB, LANES)), (0, -1, 1))

    per_row = LANES // count
    listed = partner_ref[pl.ds(rank // per_row, 1), :]
    partner = jnp.zeros((1, LANES), jnp.int32)
    for index in range(per_row):
        part_row = jnp.concatenate([listed[:, index * count : (index + 1) * count]] * SECTIONS, axis=1)
        partner = jnp.where(rank % per_row == index, part_row, partner)
    faces = [beside(face) for face in range(5)]
    picks = [
        [
            jnp.where(group == 0, faces[0][0] + (NODE1 - 1) * count, faces[1][0]),
            jnp.where(group == 0, faces[0][1], faces[1][1]),
        ],
        [jnp.where(top, low, high) + shift for low, high, shift in zip(
            faces[2], faces[3], (group * count, 0))],
        [faces[4][0] + group * count, faces[4][1]],
    ]
    index, code = found(jnp.broadcast_to(partner, (SUB, LANES)), (rotation, rotation + 1))
    picks.append([index + group * count, code])
    for kind in range(4):
        for which in range(2):
            index_ref[kind, which] = picks[kind][which]
    spread = [local + i * count for i in range(NODE1)]

    loaded(0)

    @pl.loop(0, FACE)
    def _(r):
        transposed(0, r)

    pl.semaphore_wait(barrier, len(others))
    for chunk in range(len(CHUNKS)):
        send(0, chunk)

    to_k_order(uc, uk)
    volume(uc, uk, lc, tk, 1.0)

    loaded(1)

    @pl.loop(0, FACE)
    def _(r):
        transposed(1, r)
        transposed(2, r)

    loaded(2)

    @pl.loop(0, FACE)
    def _(r):
        transposed(3, r)

    def picked(kind, values):
        index = index_ref[kind, 0]
        code = index_ref[kind, 1]
        out = take(values[0], index)
        for at_code, value in enumerate(values[1:]):
            out = jnp.where(code == at_code + 1, take(value, index), out)
        return out

    def arrived(x, chunk):
        for each in copies(x, chunk):
            each.wait_recv()

    def near_compact(x, chunk):
        first, fields = CHUNKS[chunk]
        out = []
        for each in range(fields):
            f = first + each
            low, high = [
                [y_ref[x, c_rows(f, half), :]]
                + [recv_ref[x, which, c_rows(f, half), :] for which in range(2)]
                for half in range(2)
            ]
            xs = [picked(0, low), picked(0, high)]
            y = picked(1, [pltpu.roll(jnp.where(top, a, b), NODE1, 0) for a, b in zip(low, high)])
            zs = []
            for half, values in enumerate((low, high)):
                minus = picked(2, [pltpu.roll(value, SUB - (NODE1 - 1), 0) for value in values])
                shift = NODE1 - 1 - (2 * each + half)
                packed = [zrecv_ref[x, which, chunk * SUB : (chunk + 1) * SUB, :] for which in range(2)]
                if shift:
                    packed = [pltpu.roll(value, shift, 0) for value in packed]
                plus = picked(3, packed)
                zs.append(jnp.where(k_of == 0, minus, jnp.where(k_of == NODE1 - 1, plus, 0.0)))
            out.append((f, xs, y, zs))
        return out

    def spread_near(near, put):
        for f, xs, y, zs in near:
            for side, i in enumerate((0, NODE1 - 1)):
                for half in range(2):
                    put(X_SLOT + 2 * side + half, f, take(xs[half], spread[i]))
            for i in range(NODE1):
                put(Y_SLOT + i, f, take(y, spread[i]))
                for half in range(2):
                    put(Z_SLOT + 2 * i + half, f, take(zs[half], spread[i]))

    x_side = (group == 0) | (group == NODE1 - 1)

    def lift(near, v, scale=None):
        for f, xs, y, zs in near:
            for half in range(2):
                value = jnp.where(x_side, xs[half], 0.0) + zs[half]
                value = value + jnp.where(top if half == 0 else ~top, y, 0.0)
                if scale is not None:
                    value = scale * value
                for i in range(NODE1):
                    x_ref[v, g_rows(f, i, half), :] = take(value, spread[i])

    def folded(accs):
        for bit in (1, 2, 4):
            low = (row & bit) == 0
            accs = [
                jnp.where(low, a, pltpu.roll(b, bit, 0)) + jnp.where(low, pltpu.roll(a, SUB - bit, 0), b)
                for a, b in zip(accs[::2], accs[1::2])
            ]
        return accs[0]

    def product(t, xs, dst, fields, first, last):
        vectors = len(xs)
        accs = [[None] * SUB for _ in range(vectors)]
        if not first:
            accs = [[acc_ref[v, t, a] for a in range(SUB)] for v in range(vectors)]
        for q in range(fields[0] * SUB, (fields[0] + fields[1]) * SUB):
            rows = slice(q * SUB, (q + 1) * SUB)
            parts_of = [x[rows, :] for x in xs]
            for a in range(SUB):
                m = tt_ref[t * SUB + a, rows, :]
                for v in range(vectors):
                    term = m * parts_of[v]
                    accs[v][a] = term if accs[v][a] is None else accs[v][a] + term
        for v in range(vectors):
            if last:
                dst[v][pl.ds(pl.multiple_of(t * SUB, SUB), SUB), :] = folded(accs[v])
            else:
                for a in range(SUB):
                    acc_ref[v, t, a] = accs[v][a]

    blocks = FIELDS * FACE // SUB

    def whole(xs, dst, sends, beside_of=None):
        for chunk, (first, fields) in enumerate(CHUNKS):
            @pl.loop(2 * first, 2 * (first + fields))
            def _(t):
                product(t, xs, dst, (0, FIELDS), True, True)
                if beside_of is not None and first + fields < FIELDS:
                    beside_of(t)
            for x in sends:
                send(x, chunk)

    def by_chunk(xs, dst, sends, ready):
        for chunk, fields in enumerate(CHUNKS[:-1]):
            ready(chunk)

            @pl.loop(0, blocks)
            def _(t):
                product(t, xs, dst, fields, chunk == 0, False)
        ready(len(CHUNKS) - 1)
        for chunk, (first, fields) in enumerate(CHUNKS):
            @pl.loop(2 * first, 2 * (first + fields))
            def _(t):
                product(t, xs, dst, CHUNKS[-1], False, True)
            for x in sends:
                send(x, chunk)

    def put_first(slot, f, value):
        near_ref[slot, f] = value

    for chunk in range(len(CHUNKS)):
        arrived(0, chunk)
        spread_near(near_compact(0, chunk), put_first)
    surface(uc, near_ref, lc, 1.0)

    def rest(t):
        transposed(FIELDS - 1, 2 * t)
        transposed(FIELDS - 1, 2 * t + 1)

    whole([lc], [y_ref.at[1]], [1], rest)

    def ready_v(chunk):
        arrived(1, chunk)
        near = near_compact(1, chunk)
        lift(near, 0)
        for f, xs, y, zs in near:
            for at_slot, value in enumerate((*xs, y, *zs)):
                near_v[f, at_slot] = value

    by_chunk([x_ref.at[0]], [y_ref.at[2]], [2], ready_v)

    def alpha(i):
        return time_step * sum(butcher[i])

    def coupling(i):
        return time_step * butcher[i][i] * dissipation * inv_weight

    def own(p, s):
        return p * own_sections + s % own_sections

    def per_part(value_of):
        value = jnp.float32(value_of(0))
        for other in range(1, parts):
            value = jnp.where(part == other, jnp.float32(value_of(other)), value)
        return value

    def per_lane(value_of):
        out = jnp.zeros((1, LANES), jnp.float32)
        for s in range(SECTIONS):
            out = jnp.where(block == s, per_part(lambda p, s=s: value_of(p, s)), out)
        return out

    alphas = per_lane(lambda p, s: alpha(s))
    betas = per_lane(lambda p, s: alpha(s) * coupling(s))

    for f in range(FIELDS):
        for half in range(2):
            v, w = y_ref[1, c_rows(f, half), :], y_ref[2, c_rows(f, half), :]
            for i in range(NODE1):
                rows = g_rows(f, i, half)
                vc[rows, :] = take(v, spread[i])
                wc[rows, :] = take(w, spread[i])
    gc[...] = uc[...] + alphas * vc[...] + betas * wc[...]
    to_k_order(gc, uk)
    volume(gc, uk, lc, tk, time_step)

    def add_v(slot, f, value):
        near_ref[slot, f] = near_ref[slot, f] + alphas * value

    def add_w(slot, f, value):
        near_ref[slot, f] = near_ref[slot, f] + betas * value

    for f in range(FIELDS):
        v = [near_v[f, at_slot] for at_slot in range(5)]
        spread_near([(f, v[:2], v[2], v[3:])], add_v)
    for chunk in range(len(CHUNKS)):
        arrived(2, chunk)
        spread_near(near_compact(2, chunk), add_w)
    surface(gc, near_ref, lc, time_step)

    sections = range(own_sections)
    own_alphas = [per_part(lambda p, s=s: alpha(own(p, s))) for s in sections]
    own_betas = [per_part(lambda p, s=s: alpha(own(p, s)) * coupling(own(p, s))) for s in sections]
    own_couplings = [per_part(lambda p, s=s: coupling(own(p, s))) for s in sections]
    weights = [
        [per_lane(lambda p, g, s=s, r=r: butcher[own(p, s)][(g - r) % SECTIONS]) for r in range(SECTIONS)]
        for s in sections
    ]
    tends = [lc[...]]
    for r in range(1, SECTIONS):
        tends.append(pltpu.roll(tends[0], r * count, 1))
    for s in sections:
        total = -(own_alphas[s] * vc[...] + own_betas[s] * wc[...])
        for r in range(SECTIONS):
            total = total + weights[s][r] * tends[r]
        x_ref[s] = total

    operands = [x_ref.at[s] for s in sections]
    whole(operands, [y_ref.at[3 + s] for s in sections], [3 + s for s in sections])

    def ready_first(chunk):
        for s in sections:
            arrived(3 + s, chunk)
            lift(near_compact(3 + s, chunk), s, own_couplings[s])

    by_chunk(operands, [last_ref.at[s] for s in sections], [], ready_first)

    for f in range(FIELDS):
        for half in range(2):
            rows = c_rows(f, half)
            values = [
                own_alphas[s] * y_ref[1, rows, :] + own_betas[s] * y_ref[2, rows, :]
                + y_ref[3 + s, rows, :] + last_ref[s, rows, :]
                for s in sections
            ]
            for i in range(NODE1):
                value = take(values[0], spread[i])
                for s in sections[1:]:
                    value = jnp.where(group == s, take(values[s], spread[i]), value)
                gc[g_rows(f, i, half), :] = value
    rows = gc[...].T
    for s in sections:
        out_ref[s] = rows[s * count : (s + 1) * count]
    for x in range(3 + own_sections):
        for chunk in range(len(CHUNKS)):
            for each in copies(x, chunk):
                each.wait_send()


def on_device(u_start, inverses, neighbours, partners):
    count, unknowns = u_start.shape
    devices = lax.axis_size("elem")
    own_sections = SECTIONS // lax.axis_size("section")
    listed = partners.reshape(-1, LANES)
    exchanges = 3 + own_sections
    column = pltpu.VMEM((unknowns, LANES), jnp.float32)
    compact = FIELDS * FACE
    packed = len(CHUNKS) * SUB
    vmem = pl.BlockSpec(memory_space=pltpu.VMEM)
    change = pl.pallas_call(
        functools.partial(kernel, devices, count),
        out_shape=jax.ShapeDtypeStruct((own_sections, count, unknowns), jnp.float32),
        in_specs=[pl.BlockSpec(memory_space=pl.ANY)] * 4,
        out_specs=vmem,
        scratch_shapes=[
            pltpu.VMEM(u_start.shape, jnp.float32),
            pltpu.VMEM(neighbours.shape[::-1], jnp.int32),
            pltpu.VMEM(listed.shape, jnp.int32),
            pltpu.VMEM((unknowns, count, unknowns), jnp.float32),
            pltpu.VMEM((compact, unknowns, LANES), jnp.float32),
            pltpu.VMEM((exchanges, compact, LANES), jnp.float32),
            pltpu.VMEM((exchanges, packed, LANES), jnp.float32),
            pltpu.VMEM((exchanges, 2, compact, LANES), jnp.float32),
            pltpu.VMEM((exchanges, 2, packed, LANES), jnp.float32),
            pltpu.VMEM((4, 2, SUB, LANES), jnp.int32),
            pltpu.VMEM((FIELDS, 5, SUB, LANES), jnp.float32),
            pltpu.VMEM((16, FIELDS, SUB, LANES), jnp.float32),
        ]
        + [column] * 7
        + [
            pltpu.VMEM((own_sections, unknowns, LANES), jnp.float32),
            pltpu.VMEM((own_sections, compact // SUB, SUB, SUB, LANES), jnp.float32),
            pltpu.VMEM((own_sections, compact, LANES), jnp.float32),
            pltpu.SemaphoreType.DMA((3,)),
            pltpu.SemaphoreType.DMA((len(LOADS),)),
            pltpu.SemaphoreType.DMA((exchanges, 4 * len(CHUNKS))),
            pltpu.SemaphoreType.DMA((exchanges, 4 * len(CHUNKS))),
        ],
        compiler_params=pltpu.CompilerParams(
            collective_id=0, has_side_effects=True, vmem_limit_bytes=VMEM_BYTES
        ),
    )(u_start, neighbours.T, listed, inverses)
    return u_start[None] + change


def solution(mesh):
    placed = (P("elem", None), P("elem", None, None), P("elem", None), P())
    return jax.shard_map(
        on_device, mesh=mesh, in_specs=placed, out_specs=P("section", "elem", None), check_vma=False
    )
```

time: 38 us -> 36.3 us (0.955)
  Pallas kernels: 36.3 us -> 34.6 us
    pallas_call x1, Pallas kernels: 36.3 us -> 34.6 us  [on_device(): pl.pallas_call(functools.partial(kernel, devices, count), out_shape=jax.S...]
where the time goes in v1:
time: 36.3 us; the launch traced here: 36.2 us
  Pallas kernels  34.6 us (95%)
  other arithmetic  1.54 us (4%)
    pallas_call x1, Pallas kernels, on_device(): pl.pallas_call(functools.partial(kernel, devices, count), out_shape=jax.S...  34.6 us
    add x1, other arithmetic, on_device(): return u_start[None] + change  1.54 us

profile of v1, /device:TPU:0, one launch (start us, length us, event | category | flops | bytes accessed | tf_op | source)
XLA Modules:
  0.0 36.2 jit_solution(14677832548341567547)
XLA Ops:
  0.0 0.0 copy-start
  0.0 34.6 %shard_map.46 = f32[2,32,320]{2,1,0:T(8,128)} custom-call(f32[32,320]{1,0:T(8,128)} %u_in.1, s32[5,32]{1,0:T(8,128)} %bitcast.2, s32[4,128]{1,0:T(4,128)} %bitcast.3, f32[32,320,320]{2,1,0:T(8,128)} %inv_ref.1), custom_call_target="tpu_custom_call" | custom-call | tf_op jit(solution)/shard_map/pallas_call | solution.py:645
  34.6 0.0 copy-done
  34.6 1.5 %broadcast_add_fusion = f32[2,32,320]{2,1,0:T(8,128)} fusion(f32[2,32,320]{2,1,0:T(8,128)} %shard_map.46, f32[32,320]{1,0:T(8,128)S(1)} %copy-done), kind=kLoop, calls=%fused_computation | loop fusion | flops 20480 | bytes 204800 | tf_op jit(solution)/shard_map/add | solution.py:678
Async XLA Ops:
  0.0 34.6 %copy-start = (f32[32,320]{1,0:T(8,128)S(1)}, f32[32,320]{1,0:T(8,128)}, u32[]{:S(2)}) copy-start(f32[32,320]{1,0:T(8,128)} %u_in.1) | copy-start | bytes 122884

commit v2 on v1

--- a/solution.py
+++ b/solution.py
@@ -85,6 +85,8 @@
 LANES = 128
 SUB = 8
 CHUNKS = ((0, 2), (2, 2), (4, 1))
+WHOLE = (0, 0, 0)
+SPLIT = (0, 1, 2)
 LOADS = ((0, 1), (1, 2), (3, 2))
 X_SLOT, Y_SLOT, Z_SLOT = 0, 4, 8
 VMEM_BYTES = 54 * 2**20
@@ -230,9 +232,9 @@
 def kernel(
     devices, count, u_in, nbr_in, partner_in, inv_ref, out_ref,
     u_ref, nbr_ref, partner_ref,
-    raw_ref, tt_ref, y_ref, zsend_ref, recv_ref, zrecv_ref, index_ref, near_v, near_ref,
-    uc, uk, vc, wc, lc, tk, gc, x_ref, acc_ref, last_ref,
-    in_sem, a_sem, send_sem, recv_sem,
+    raw_ref, tt_ref, y_ref, zsend_ref, recv_ref, zrecv_ref, index_ref, near_v, near_z, near_ref,
+    uc, uk, vc, wc, lc, tk, gc, x_ref, acc_ref, last_ref, done_ref,
+    in_sem, a_sem, send_sem, recv_sem, out_sem,
 ):
     rank = lax.axis_index("elem")
     part = lax.axis_index("section")
@@ -286,6 +288,12 @@
     k_of = row % NODE1
     block = group[:1]
 
+    events = [(0, WHOLE), (1, SPLIT), (4, WHOLE)] + [(5, SPLIT)] * own_sections
+
+    def event(x, chunk):
+        base, offsets = events[x]
+        return base + offsets[chunk]
+
     def copies(x, chunk):
         first, fields = CHUNKS[chunk]
         rows = pl.ds(first * FACE, fields * FACE)
@@ -298,24 +306,32 @@
             else:
                 src, dst = zsend_ref.at[x, zrows], zrecv_ref.at[x, which - 2, zrows]
                 target = at(-rotation) if which == 2 else at(-rotation - 1)
-            slot = chunk * 4 + which
             out.append(pltpu.make_async_remote_copy(
-                src_ref=src, dst_ref=dst, send_sem=send_sem.at[x, slot],
-                recv_sem=recv_sem.at[x, slot], device_id={"elem": target}, device_id_type=MESH,
+                src_ref=src, dst_ref=dst, send_sem=send_sem.at[which // 2],
+                recv_sem=recv_sem.at[event(x, chunk)], device_id={"elem": target}, device_id_type=MESH,
             ))
         return out
 
-    def pack(x, chunk):
+    def arrived(xs, chunks):
+        rows = sum(2 * CHUNKS[chunk][1] * FACE + 2 * SUB for chunk in chunks) * len(xs)
+        there = tt_ref.at[0, pl.ds(0, rows)]
+        pltpu.make_async_copy(there, there, recv_sem.at[event(xs[0], chunks[0])]).wait()
+
+    def packed_rows(values, k):
+        packed = jnp.zeros((SUB, LANES), jnp.float32)
+        for slot, value in enumerate(values):
+            shift = (slot - k) % SUB
+            value = pltpu.roll(value, shift, 0) if shift else value
+            packed = jnp.where(k_of == slot, value, packed)
+        return packed
+
+    def chunk_rows(chunk):
         first, fields = CHUNKS[chunk]
-        packed = jnp.zeros((SUB, LANES), jnp.float32)
-        for slot in range(2 * fields):
-            value = y_ref[x, c_rows(first + slot // 2, slot % 2), :]
-            value = value if slot == 0 else pltpu.roll(value, slot, 0)
-            packed = jnp.where(k_of == slot, value, packed)
+        return [c_rows(first + slot // 2, slot % 2) for slot in range(2 * fields)]
+
+    def send(x, chunk):
+        packed = packed_rows([y_ref[x, rows, :] for rows in chunk_rows(chunk)], 0)
         zsend_ref[x, chunk * SUB : (chunk + 1) * SUB, :] = packed
-
-    def send(x, chunk):
-        pack(x, chunk)
         out = copies(x, chunk)
         for which in (3, 2, 0, 1):
             out[which].start()
@@ -368,33 +384,18 @@
     for kind in range(4):
         for which in range(2):
             index_ref[kind, which] = picks[kind][which]
-    spread = [local + i * count for i in range(NODE1)]
-
-    loaded(0)
-
-    @pl.loop(0, FACE)
-    def _(r):
-        transposed(0, r)
-
     pl.semaphore_wait(barrier, len(others))
     for chunk in range(len(CHUNKS)):
         send(0, chunk)
 
+    for part_of, (first, fields) in enumerate(LOADS):
+        loaded(part_of)
+        for f in range(first, first + fields):
+            for r in range(FACE):
+                transposed(f, r)
+
     to_k_order(uc, uk)
     volume(uc, uk, lc, tk, 1.0)
-
-    loaded(1)
-
-    @pl.loop(0, FACE)
-    def _(r):
-        transposed(1, r)
-        transposed(2, r)
-
-    loaded(2)
-
-    @pl.loop(0, FACE)
-    def _(r):
-        transposed(3, r)
 
     def picked(kind, values):
         index = index_ref[kind, 0]
@@ -404,55 +405,71 @@
             out = jnp.where(code == at_code + 1, take(value, index), out)
         return out
 
-    def arrived(x, chunk):
-        for each in copies(x, chunk):
-            each.wait_recv()
-
     def near_compact(x, chunk):
         first, fields = CHUNKS[chunk]
-        out = []
-        for each in range(fields):
-            f = first + each
+        sides = []
+        for f in range(first, first + fields):
             low, high = [
                 [y_ref[x, c_rows(f, half), :]]
                 + [recv_ref[x, which, c_rows(f, half), :] for which in range(2)]
                 for half in range(2)
             ]
-            xs = [picked(0, low), picked(0, high)]
             y = picked(1, [pltpu.roll(jnp.where(top, a, b), NODE1, 0) for a, b in zip(low, high)])
-            zs = []
-            for half, values in enumerate((low, high)):
-                minus = picked(2, [pltpu.roll(value, SUB - (NODE1 - 1), 0) for value in values])
-                shift = NODE1 - 1 - (2 * each + half)
-                packed = [zrecv_ref[x, which, chunk * SUB : (chunk + 1) * SUB, :] for which in range(2)]
-                if shift:
-                    packed = [pltpu.roll(value, shift, 0) for value in packed]
-                plus = picked(3, packed)
-                zs.append(jnp.where(k_of == 0, minus, jnp.where(k_of == NODE1 - 1, plus, 0.0)))
-            out.append((f, xs, y, zs))
+            sides.append((picked(0, low), picked(0, high), y))
+        there = chunk_rows(chunk)
+        minus = [packed_rows([y_ref[x, rows, :] for rows in there], NODE1 - 1)]
+        for which in range(2):
+            minus.append(packed_rows([recv_ref[x, which, rows, :] for rows in there], NODE1 - 1))
+        plus = [zrecv_ref[x, which, chunk * SUB : (chunk + 1) * SUB, :] for which in range(2)]
+        return sides, picked(2, minus), picked(3, plus)
+
+    def spread(value):
+        turned = [value] + [pltpu.roll(value, i * count, 1) for i in range(1, NODE1)]
+        out = []
+        for i in range(NODE1):
+            each = turned[(NODE1 - 1 - i) % NODE1]
+            for c in range(NODE1 - 2, -1, -1):
+                each = jnp.where(group == c, turned[(c - i) % NODE1], each)
+            out.append(each)
         return out
 
-    def spread_near(near, put):
-        for f, xs, y, zs in near:
-            for side, i in enumerate((0, NODE1 - 1)):
+    def z_state(minus, plus, slot):
+        if slot:
+            minus = pltpu.roll(minus, SUB - slot, 0)
+        if slot != NODE1 - 1:
+            plus = pltpu.roll(plus, NODE1 - 1 - slot, 0)
+        return jnp.where(k_of == 0, minus, jnp.where(k_of == NODE1 - 1, plus, 0.0))
+
+    def spread_near(chunk, near, put):
+        sides, minus, plus = near
+        minus, plus = spread(minus), spread(plus)
+        first, fields = CHUNKS[chunk]
+        for each, (x_low, x_high, y) in enumerate(sides):
+            f = first + each
+            for half, value in enumerate((x_low, x_high)):
+                out = spread(value)
+                for side, i in enumerate((0, NODE1 - 1)):
+                    put(X_SLOT + 2 * side + half, f, out[i])
+            out = spread(y)
+            for i in range(NODE1):
+                put(Y_SLOT + i, f, out[i])
                 for half in range(2):
-                    put(X_SLOT + 2 * side + half, f, take(xs[half], spread[i]))
-            for i in range(NODE1):
-                put(Y_SLOT + i, f, take(y, spread[i]))
-                for half in range(2):
-                    put(Z_SLOT + 2 * i + half, f, take(zs[half], spread[i]))
+                    put(Z_SLOT + 2 * i + half, f, z_state(minus[i], plus[i], 2 * each + half))
 
     x_side = (group == 0) | (group == NODE1 - 1)
 
-    def lift(near, v, scale=None):
-        for f, xs, y, zs in near:
-            for half in range(2):
-                value = jnp.where(x_side, xs[half], 0.0) + zs[half]
+    def lift(chunk, near, v, scale=None):
+        sides, minus, plus = near
+        first, fields = CHUNKS[chunk]
+        for each, (x_low, x_high, y) in enumerate(sides):
+            for half, value in enumerate((x_low, x_high)):
+                value = jnp.where(x_side, value, 0.0) + z_state(minus, plus, 2 * each + half)
                 value = value + jnp.where(top if half == 0 else ~top, y, 0.0)
                 if scale is not None:
                     value = scale * value
+                out = spread(value)
                 for i in range(NODE1):
-                    x_ref[v, g_rows(f, i, half), :] = take(value, spread[i])
+                    x_ref[v, g_rows(first + each, i, half), :] = out[i]
 
     def folded(accs):
         for bit in (1, 2, 4):
@@ -485,13 +502,12 @@
 
     blocks = FIELDS * FACE // SUB
 
-    def whole(xs, dst, sends, beside_of=None):
+    def whole(xs, dst, sends):
         for chunk, (first, fields) in enumerate(CHUNKS):
             @pl.loop(2 * first, 2 * (first + fields))
             def _(t):
                 product(t, xs, dst, (0, FIELDS), True, True)
-                if beside_of is not None and first + fields < FIELDS:
-                    beside_of(t)
+
             for x in sends:
                 send(x, chunk)
 
@@ -513,24 +529,23 @@
     def put_first(slot, f, value):
         near_ref[slot, f] = value
 
-    for chunk in range(len(CHUNKS)):
-        arrived(0, chunk)
-        spread_near(near_compact(0, chunk), put_first)
+    every = range(len(CHUNKS))
+    arrived([0], every)
+    for chunk in every:
+        spread_near(chunk, near_compact(0, chunk), put_first)
     surface(uc, near_ref, lc, 1.0)
-
-    def rest(t):
-        transposed(FIELDS - 1, 2 * t)
-        transposed(FIELDS - 1, 2 * t + 1)
-
-    whole([lc], [y_ref.at[1]], [1], rest)
+    whole([lc], [y_ref.at[1]], [1])
 
     def ready_v(chunk):
-        arrived(1, chunk)
+        arrived([1], [chunk])
         near = near_compact(1, chunk)
-        lift(near, 0)
-        for f, xs, y, zs in near:
-            for at_slot, value in enumerate((*xs, y, *zs)):
-                near_v[f, at_slot] = value
+        lift(chunk, near, 0)
+        sides, minus, plus = near
+        for each, side in enumerate(sides):
+            for slot, value in enumerate(side):
+                near_v[CHUNKS[chunk][0] + each, slot] = value
+        near_z[chunk, 0] = minus
+        near_z[chunk, 1] = plus
 
     by_chunk([x_ref.at[0]], [y_ref.at[2]], [2], ready_v)
 
@@ -561,10 +576,10 @@
     for f in range(FIELDS):
         for half in range(2):
             v, w = y_ref[1, c_rows(f, half), :], y_ref[2, c_rows(f, half), :]
-            for i in range(NODE1):
+            for i, (v, w) in enumerate(zip(spread(v), spread(w))):
                 rows = g_rows(f, i, half)
-                vc[rows, :] = take(v, spread[i])
-                wc[rows, :] = take(w, spread[i])
+                vc[rows, :] = v
+                wc[rows, :] = w
     gc[...] = uc[...] + alphas * vc[...] + betas * wc[...]
     to_k_order(gc, uk)
     volume(gc, uk, lc, tk, time_step)
@@ -575,12 +590,12 @@
     def add_w(slot, f, value):
         near_ref[slot, f] = near_ref[slot, f] + betas * value
 
-    for f in range(FIELDS):
-        v = [near_v[f, at_slot] for at_slot in range(5)]
-        spread_near([(f, v[:2], v[2], v[3:])], add_v)
-    for chunk in range(len(CHUNKS)):
-        arrived(2, chunk)
-        spread_near(near_compact(2, chunk), add_w)
+    for chunk, (first, fields) in enumerate(CHUNKS):
+        sides = [[near_v[f, slot] for slot in range(3)] for f in range(first, first + fields)]
+        spread_near(chunk, (sides, near_z[chunk, 0], near_z[chunk, 1]), add_v)
+    arrived([2], every)
+    for chunk in every:
+        spread_near(chunk, near_compact(2, chunk), add_w)
     surface(gc, near_ref, lc, time_step)
 
     sections = range(own_sections)
@@ -604,9 +619,9 @@
     whole(operands, [y_ref.at[3 + s] for s in sections], [3 + s for s in sections])
 
     def ready_first(chunk):
+        arrived([3 + s for s in sections], [chunk])
         for s in sections:
-            arrived(3 + s, chunk)
-            lift(near_compact(3 + s, chunk), s, own_couplings[s])
+            lift(chunk, near_compact(3 + s, chunk), s, own_couplings[s])
 
     by_chunk(operands, [last_ref.at[s] for s in sections], [], ready_first)
 
@@ -618,18 +633,20 @@
                 + y_ref[3 + s, rows, :] + last_ref[s, rows, :]
                 for s in sections
             ]
+            values = [spread(value) for value in values]
             for i in range(NODE1):
-                value = take(values[0], spread[i])
+                value = values[0][i]
                 for s in sections[1:]:
-                    value = jnp.where(group == s, take(values[s], spread[i]), value)
+                    value = jnp.where(group == s, values[s][i], value)
                 gc[g_rows(f, i, half), :] = value
     rows = gc[...].T
     for s in sections:
-        out_ref[s] = rows[s * count : (s + 1) * count]
-    for x in range(3 + own_sections):
-        for chunk in range(len(CHUNKS)):
-            for each in copies(x, chunk):
-                each.wait_send()
+        done_ref[s] = rows[s * count : (s + 1) * count]
+    out = pltpu.make_async_copy(done_ref, out_ref, out_sem)
+    out.start()
+    for which, there in enumerate((recv_ref, zrecv_ref)):
+        pltpu.make_async_copy(there, there, send_sem.at[which]).wait()
+    out.wait()
 
 
 def on_device(u_start, inverses, neighbours, partners):
@@ -641,12 +658,11 @@
     column = pltpu.VMEM((unknowns, LANES), jnp.float32)
     compact = FIELDS * FACE
     packed = len(CHUNKS) * SUB
-    vmem = pl.BlockSpec(memory_space=pltpu.VMEM)
     change = pl.pallas_call(
         functools.partial(kernel, devices, count),
         out_shape=jax.ShapeDtypeStruct((own_sections, count, unknowns), jnp.float32),
         in_specs=[pl.BlockSpec(memory_space=pl.ANY)] * 4,
-        out_specs=vmem,
+        out_specs=pl.BlockSpec(memory_space=pl.ANY),
         scratch_shapes=[
             pltpu.VMEM(u_start.shape, jnp.float32),
             pltpu.VMEM(neighbours.shape[::-1], jnp.int32),
@@ -658,7 +674,8 @@
             pltpu.VMEM((exchanges, 2, compact, LANES), jnp.float32),
             pltpu.VMEM((exchanges, 2, packed, LANES), jnp.float32),
             pltpu.VMEM((4, 2, SUB, LANES), jnp.int32),
-            pltpu.VMEM((FIELDS, 5, SUB, LANES), jnp.float32),
+            pltpu.VMEM((FIELDS, 3, SUB, LANES), jnp.float32),
+            pltpu.VMEM((len(CHUNKS), 2, SUB, LANES), jnp.float32),
             pltpu.VMEM((16, FIELDS, SUB, LANES), jnp.float32),
         ]
         + [column] * 7
@@ -666,10 +683,12 @@
             pltpu.VMEM((own_sections, unknowns, LANES), jnp.float32),
             pltpu.VMEM((own_sections, compact // SUB, SUB, SUB, LANES), jnp.float32),
             pltpu.VMEM((own_sections, compact, LANES), jnp.float32),
+            pltpu.VMEM((own_sections, count, unknowns), jnp.float32),
             pltpu.SemaphoreType.DMA((3,)),
             pltpu.SemaphoreType.DMA((len(LOADS),)),
-            pltpu.SemaphoreType.DMA((exchanges, 4 * len(CHUNKS))),
-            pltpu.SemaphoreType.DMA((exchanges, 4 * len(CHUNKS))),
+            pltpu.SemaphoreType.DMA((2,)),
+            pltpu.SemaphoreType.DMA((8,)),
+            pltpu.SemaphoreType.DMA,
         ],
         compiler_params=pltpu.CompilerParams(
             collective_id=0, has_side_effects=True, vmem_limit_bytes=VMEM_BYTES

time: 36.3 us -> 32.5 us (0.90)
  Pallas kernels: 34.6 us -> 30.8 us
    pallas_call x1, Pallas kernels: 34.6 us -> 30.8 us  [on_device(): pl.pallas_call(functools.partial(kernel, devices, count), out_shape=jax.S...]
where the time goes in v2:
time: 32.5 us; the launch traced here: 32.4 us
  Pallas kernels  30.8 us (95%)
  other arithmetic  1.54 us (5%)
    pallas_call x1, Pallas kernels, on_device(): pl.pallas_call(functools.partial(kernel, devices, count), out_shape=jax.S...  30.8 us
    add x1, other arithmetic, on_device(): return u_start[None] + change  1.54 us

profile of v2, /device:TPU:0, one launch (start us, length us, event | category | flops | bytes accessed | tf_op | source)
XLA Modules:
  0.0 32.4 jit_solution(12426921273094396713)
XLA Ops:
  0.0 0.0 copy-start
  0.0 30.8 %shard_map.46 = f32[2,32,320]{2,1,0:T(8,128)} custom-call(f32[32,320]{1,0:T(8,128)} %u_in.1, s32[5,32]{1,0:T(8,128)} %bitcast.2, s32[4,128]{1,0:T(4,128)} %bitcast.3, f32[32,320,320]{2,1,0:T(8,128)} %inv_ref.1), custom_call_target="tpu_custom_call" | custom-call | tf_op jit(solution)/shard_map/pallas_call | solution.py:661
  30.8 0.0 copy-done
  30.8 1.5 %broadcast_add_fusion = f32[2,32,320]{2,1,0:T(8,128)} fusion(f32[2,32,320]{2,1,0:T(8,128)} %shard_map.46, f32[32,320]{1,0:T(8,128)S(1)} %copy-done), kind=kLoop, calls=%fused_computation | loop fusion | flops 20480 | bytes 204800 | tf_op jit(solution)/shard_map/add | solution.py:697
Async XLA Ops:
  0.0 30.8 %copy-start = (f32[32,320]{1,0:T(8,128)S(1)}, f32[32,320]{1,0:T(8,128)}, u32[]{:S(2)}) copy-start(f32[32,320]{1,0:T(8,128)} %u_in.1) | copy-start | bytes 122884

commit v3 on v2

--- a/solution.py
+++ b/solution.py
@@ -87,7 +87,7 @@
 CHUNKS = ((0, 2), (2, 2), (4, 1))
 WHOLE = (0, 0, 0)
 SPLIT = (0, 1, 2)
-LOADS = ((0, 1), (1, 2), (3, 2))
+LOADS = tuple((f, 1) for f in range(5))
 X_SLOT, Y_SLOT, Z_SLOT = 0, 4, 8
 VMEM_BYTES = 54 * 2**20
 MESH = pl.DeviceIdType.MESH
@@ -233,8 +233,8 @@
     devices, count, u_in, nbr_in, partner_in, inv_ref, out_ref,
     u_ref, nbr_ref, partner_ref,
     raw_ref, tt_ref, y_ref, zsend_ref, recv_ref, zrecv_ref, index_ref, near_v, near_z, near_ref,
-    uc, uk, vc, wc, lc, tk, gc, x_ref, acc_ref, last_ref, done_ref,
-    in_sem, a_sem, send_sem, recv_sem, out_sem,
+    uc, uk, vc, wc, lc, tk, gc, x_ref, acc_ref, last_ref,
+    in_sem, a_sem, send_sem, recv_sem,
 ):
     rank = lax.axis_index("elem")
     part = lax.axis_index("section")
@@ -279,6 +279,7 @@
             tt_ref[f * FACE + r, q : q + width, :] = jnp.concatenate(blocks, axis=0).T
 
     load(0)
+    load(1)
 
     row = lax.broadcasted_iota(jnp.int32, (SUB, LANES), 0)
     lane = lax.broadcasted_iota(jnp.int32, (SUB, LANES), 1)
@@ -333,7 +334,7 @@
         packed = packed_rows([y_ref[x, rows, :] for rows in chunk_rows(chunk)], 0)
         zsend_ref[x, chunk * SUB : (chunk + 1) * SUB, :] = packed
         out = copies(x, chunk)
-        for which in (3, 2, 0, 1):
+        for which in (0, 1, 3, 2):
             out[which].start()
 
     for each in small:
@@ -346,8 +347,8 @@
                 value = jnp.where(group == i, uc[g_rows(f, i, half), :], value)
             y_ref[0, c_rows(f, half), :] = value
 
-    load(1)
-    load(2)
+    for part_of in range(2, len(LOADS)):
+        load(part_of)
 
     def found(wanted, offsets):
         index = wanted - at(offsets[0]) * count
@@ -384,16 +385,18 @@
     for kind in range(4):
         for which in range(2):
             index_ref[kind, which] = picks[kind][which]
+    loaded(0)
+    for r in range(FACE // 2):
+        transposed(0, r)
     pl.semaphore_wait(barrier, len(others))
     for chunk in range(len(CHUNKS)):
         send(0, chunk)
-
-    for part_of, (first, fields) in enumerate(LOADS):
-        loaded(part_of)
-        for f in range(first, first + fields):
-            for r in range(FACE):
-                transposed(f, r)
-
+    for r in range(FACE // 2, FACE):
+        transposed(0, r)
+    for f in range(1, FIELDS):
+        loaded(f)
+        for r in range(FACE):
+            transposed(f, r)
     to_k_order(uc, uk)
     volume(uc, uk, lc, tk, 1.0)
 
@@ -511,14 +514,14 @@
             for x in sends:
                 send(x, chunk)
 
-    def by_chunk(xs, dst, sends, ready):
+    def by_chunk(xs, dst, sends, await_chunk, ready):
+        await_chunk(0)
+        ready(0)
         for chunk, fields in enumerate(CHUNKS[:-1]):
-            ready(chunk)
-
-            @pl.loop(0, blocks)
-            def _(t):
+            await_chunk(chunk + 1)
+            ready(chunk + 1)
+            for t in range(blocks):
                 product(t, xs, dst, fields, chunk == 0, False)
-        ready(len(CHUNKS) - 1)
         for chunk, (first, fields) in enumerate(CHUNKS):
             @pl.loop(2 * first, 2 * (first + fields))
             def _(t):
@@ -537,7 +540,6 @@
     whole([lc], [y_ref.at[1]], [1])
 
     def ready_v(chunk):
-        arrived([1], [chunk])
         near = near_compact(1, chunk)
         lift(chunk, near, 0)
         sides, minus, plus = near
@@ -547,7 +549,7 @@
         near_z[chunk, 0] = minus
         near_z[chunk, 1] = plus
 
-    by_chunk([x_ref.at[0]], [y_ref.at[2]], [2], ready_v)
+    by_chunk([x_ref.at[0]], [y_ref.at[2]], [2], lambda chunk: arrived([1], [chunk]), ready_v)
 
     def alpha(i):
         return time_step * sum(butcher[i])
@@ -593,11 +595,6 @@
     for chunk, (first, fields) in enumerate(CHUNKS):
         sides = [[near_v[f, slot] for slot in range(3)] for f in range(first, first + fields)]
         spread_near(chunk, (sides, near_z[chunk, 0], near_z[chunk, 1]), add_v)
-    arrived([2], every)
-    for chunk in every:
-        spread_near(chunk, near_compact(2, chunk), add_w)
-    surface(gc, near_ref, lc, time_step)
-
     sections = range(own_sections)
     own_alphas = [per_part(lambda p, s=s: alpha(own(p, s))) for s in sections]
     own_betas = [per_part(lambda p, s=s: alpha(own(p, s)) * coupling(own(p, s))) for s in sections]
@@ -606,24 +603,34 @@
         [per_lane(lambda p, g, s=s, r=r: butcher[own(p, s)][(g - r) % SECTIONS]) for r in range(SECTIONS)]
         for s in sections
     ]
-    tends = [lc[...]]
-    for r in range(1, SECTIONS):
-        tends.append(pltpu.roll(tends[0], r * count, 1))
     for s in sections:
-        total = -(own_alphas[s] * vc[...] + own_betas[s] * wc[...])
-        for r in range(SECTIONS):
-            total = total + weights[s][r] * tends[r]
-        x_ref[s] = total
+        x_ref[s] = -(own_alphas[s] * vc[...] + own_betas[s] * wc[...])
+    arrived([2], every)
+    for chunk in every:
+        spread_near(chunk, near_compact(2, chunk), add_w)
+    surface(gc, near_ref, lc, time_step)
+
+    for start in range(0, unknowns, SUB):
+        rows = slice(start, start + SUB)
+        tend = lc[rows, :]
+        turned = [tend] + [pltpu.roll(tend, r * count, 1) for r in range(1, SECTIONS)]
+        for s in sections:
+            total = x_ref[s, rows, :]
+            for r in range(SECTIONS):
+                total = total + weights[s][r] * turned[r]
+            x_ref[s, rows, :] = total
 
     operands = [x_ref.at[s] for s in sections]
     whole(operands, [y_ref.at[3 + s] for s in sections], [3 + s for s in sections])
 
+    def await_first(chunk):
+        arrived([3 + s for s in sections], [chunk])
+
     def ready_first(chunk):
-        arrived([3 + s for s in sections], [chunk])
         for s in sections:
             lift(chunk, near_compact(3 + s, chunk), s, own_couplings[s])
 
-    by_chunk(operands, [last_ref.at[s] for s in sections], [], ready_first)
+    by_chunk(operands, [last_ref.at[s] for s in sections], [], await_first, ready_first)
 
     for f in range(FIELDS):
         for half in range(2):
@@ -641,12 +648,9 @@
                 gc[g_rows(f, i, half), :] = value
     rows = gc[...].T
     for s in sections:
-        done_ref[s] = rows[s * count : (s + 1) * count]
-    out = pltpu.make_async_copy(done_ref, out_ref, out_sem)
-    out.start()
+        out_ref[s] = rows[s * count : (s + 1) * count]
     for which, there in enumerate((recv_ref, zrecv_ref)):
         pltpu.make_async_copy(there, there, send_sem.at[which]).wait()
-    out.wait()
 
 
 def on_device(u_start, inverses, neighbours, partners):
@@ -660,9 +664,9 @@
     packed = len(CHUNKS) * SUB
     change = pl.pallas_call(
         functools.partial(kernel, devices, count),
-        out_shape=jax.ShapeDtypeStruct((own_sections, count, unknowns), jnp.float32),
+        out_shape=pltpu.VMEM((own_sections, count, unknowns), jnp.float32),
         in_specs=[pl.BlockSpec(memory_space=pl.ANY)] * 4,
-        out_specs=pl.BlockSpec(memory_space=pl.ANY),
+        out_specs=pl.BlockSpec(memory_space=pltpu.VMEM),
         scratch_shapes=[
             pltpu.VMEM(u_start.shape, jnp.float32),
             pltpu.VMEM(neighbours.shape[::-1], jnp.int32),
@@ -683,12 +687,10 @@
             pltpu.VMEM((own_sections, unknowns, LANES), jnp.float32),
             pltpu.VMEM((own_sections, compact // SUB, SUB, SUB, LANES), jnp.float32),
             pltpu.VMEM((own_sections, compact, LANES), jnp.float32),
-            pltpu.VMEM((own_sections, count, unknowns), jnp.float32),
             pltpu.SemaphoreType.DMA((3,)),
             pltpu.SemaphoreType.DMA((len(LOADS),)),
             pltpu.SemaphoreType.DMA((2,)),
             pltpu.SemaphoreType.DMA((8,)),
-            pltpu.SemaphoreType.DMA,
         ],
         compiler_params=pltpu.CompilerParams(
             collective_id=0, has_side_effects=True, vmem_limit_bytes=VMEM_BYTES

time: 32.5 us -> 29.9 us (0.920)
  Pallas kernels: 30.8 us -> 29.1 us
  other arithmetic: 1.54 us -> 0.65 us
    pallas_call x1, Pallas kernels: 30.8 us -> 29.1 us  [on_device(): pl.pallas_call(functools.partial(kernel, devices, count), out_shape=pltpu...]
    add x1, other arithmetic: 1.54 us -> 0.65 us  [on_device(): return u_start[None] + change]
where the time goes in v3:
time: 29.9 us; the launch traced here: 29.8 us
  Pallas kernels  29.1 us (97%)
  other arithmetic  0.65 us (2%)
    pallas_call x1, Pallas kernels, on_device(): pl.pallas_call(functools.partial(kernel, devices, count), out_shape=pltpu...  29.1 us
    add x1, other arithmetic, on_device(): return u_start[None] + change  0.65 us

profile of v3, /device:TPU:0, one launch (start us, length us, event | category | flops | bytes accessed | tf_op | source)
XLA Modules:
  0.0 29.8 jit_solution(17980403991288613171)
XLA Ops:
  0.0 0.0 copy-start
  0.0 29.1 %shard_map.46 = f32[2,32,320]{2,1,0:T(8,128)S(1)} custom-call(f32[32,320]{1,0:T(8,128)} %u_in.1, s32[5,32]{1,0:T(8,128)} %bitcast.2, s32[4,128]{1,0:T(4,128)} %bitcast.3, f32[32,320,320]{2,1,0:T(8,128)} %inv_ref.1), custom_call_target="tpu_custom_call" | custom-call | tf_op jit(solution)/shard_map/pallas_call | solution.py:665
  29.1 0.0 copy-done
  29.1 0.7 %broadcast_add_fusion = f32[2,32,320]{2,1,0:T(8,128)} fusion(f32[2,32,320]{2,1,0:T(8,128)S(1)} %shard_map.46, f32[32,320]{1,0:T(8,128)S(1)} %copy-done), kind=kLoop, calls=%fused_computation | loop fusion | flops 20480 | bytes 204800 | tf_op jit(solution)/shard_map/add | solution.py:699
Async XLA Ops:
  0.0 29.1 %copy-start = (f32[32,320]{1,0:T(8,128)S(1)}, f32[32,320]{1,0:T(8,128)}, u32[]{:S(2)}) copy-start(f32[32,320]{1,0:T(8,128)} %u_in.1) | copy-start | bytes 122884

commit v4 on v3

--- a/solution.py
+++ b/solution.py
@@ -85,8 +85,8 @@
 LANES = 128
 SUB = 8
 CHUNKS = ((0, 2), (2, 2), (4, 1))
-WHOLE = (0, 0, 0)
-SPLIT = (0, 1, 2)
+FINE = tuple((f, 1) for f in range(5))
+SPLIT_AT = 10
 LOADS = tuple((f, 1) for f in range(5))
 X_SLOT, Y_SLOT, Z_SLOT = 0, 4, 8
 VMEM_BYTES = 54 * 2**20
@@ -221,6 +221,10 @@
     return slice(start, start + SUB)
 
 
+def chunks_of(x):
+    return FINE if x > 2 else CHUNKS
+
+
 def near_state(near_ref, slot):
     return [near_ref[slot, f] for f in range(FIELDS)]
 
@@ -232,8 +236,8 @@
 def kernel(
     devices, count, u_in, nbr_in, partner_in, inv_ref, out_ref,
     u_ref, nbr_ref, partner_ref,
-    raw_ref, tt_ref, y_ref, zsend_ref, recv_ref, zrecv_ref, index_ref, near_v, near_z, near_ref,
-    uc, uk, vc, wc, lc, tk, gc, x_ref, acc_ref, last_ref,
+    raw_ref, tt_ref, y_ref, zsend_ref, recv_ref, zrecv_ref, index_ref, near_v, near_z, near_ref, own_ref, own_z,
+    uc, uk, vc, wc, lc, tk, gc, x_ref, acc_ref, last_ref, eye_ref,
     in_sem, a_sem, send_sem, recv_sem,
 ):
     rank = lax.axis_index("elem")
@@ -278,6 +282,27 @@
             blocks = [raw_ref[f * NODES + b * FACE + r, :, q : q + width] for b in range(NODE1)]
             tt_ref[f * FACE + r, q : q + width, :] = jnp.concatenate(blocks, axis=0).T
 
+    def transposed_pair(f, r):
+        rows_of = (((1,), (1,)), ((), ()))
+        for q in range(0, unknowns, LANES):
+            width = min(LANES, unknowns - q)
+            blocks = [
+                raw_ref[f * NODES + b * FACE + r + each, :, q : q + width]
+                for each in range(2) for b in range(NODE1)
+            ]
+            both = jnp.concatenate(blocks, axis=0)
+            high = both.astype(jnp.bfloat16)
+            low = (both - high.astype(jnp.float32)).astype(jnp.bfloat16)
+            if width == LANES:
+                halves = jnp.concatenate([high, low], axis=1)
+                out = lax.dot_general(eye_ref[...], halves, rows_of, preferred_element_type=jnp.float32)
+            else:
+                eye = eye_ref[:width, :width]
+                out = lax.dot_general(eye, high, rows_of, preferred_element_type=jnp.float32)
+                out = out + lax.dot_general(eye, low, rows_of, preferred_element_type=jnp.float32)
+            for each in range(2):
+                tt_ref[f * FACE + r + each, q : q + width, :] = out[:, each * LANES : (each + 1) * LANES]
+
     load(0)
     load(1)
 
@@ -289,14 +314,13 @@
     k_of = row % NODE1
     block = group[:1]
 
-    events = [(0, WHOLE), (1, SPLIT), (4, WHOLE)] + [(5, SPLIT)] * own_sections
-
     def event(x, chunk):
-        base, offsets = events[x]
-        return base + offsets[chunk]
+        if x == 0:
+            return 0
+        return 1 + chunk + (min(x, 3) - 1) * len(CHUNKS)
 
     def copies(x, chunk):
-        first, fields = CHUNKS[chunk]
+        first, fields = chunks_of(x)[chunk]
         rows = pl.ds(first * FACE, fields * FACE)
         zrows = pl.ds(chunk * SUB, SUB)
         out = []
@@ -314,7 +338,7 @@
         return out
 
     def arrived(xs, chunks):
-        rows = sum(2 * CHUNKS[chunk][1] * FACE + 2 * SUB for chunk in chunks) * len(xs)
+        rows = sum(2 * chunks_of(xs[0])[chunk][1] * FACE + 2 * SUB for chunk in chunks) * len(xs)
         there = tt_ref.at[0, pl.ds(0, rows)]
         pltpu.make_async_copy(there, there, recv_sem.at[event(xs[0], chunks[0])]).wait()
 
@@ -326,12 +350,12 @@
             packed = jnp.where(k_of == slot, value, packed)
         return packed
 
-    def chunk_rows(chunk):
-        first, fields = CHUNKS[chunk]
+    def chunk_rows(x, chunk):
+        first, fields = chunks_of(x)[chunk]
         return [c_rows(first + slot // 2, slot % 2) for slot in range(2 * fields)]
 
     def send(x, chunk):
-        packed = packed_rows([y_ref[x, rows, :] for rows in chunk_rows(chunk)], 0)
+        packed = packed_rows([y_ref[x, rows, :] for rows in chunk_rows(x, chunk)], 0)
         zsend_ref[x, chunk * SUB : (chunk + 1) * SUB, :] = packed
         out = copies(x, chunk)
         for which in (0, 1, 3, 2):
@@ -385,46 +409,59 @@
     for kind in range(4):
         for which in range(2):
             index_ref[kind, which] = picks[kind][which]
-    loaded(0)
-    for r in range(FACE // 2):
-        transposed(0, r)
+    def picked(kind, own, values):
+        index = index_ref[kind, 0]
+        code = index_ref[kind, 1]
+        for at_code, value in enumerate(values):
+            own = jnp.where(code == at_code + 1, take(value, index), own)
+        return own
+
+    def crossed(low, high):
+        return pltpu.roll(jnp.where(top, low, high), NODE1, 0)
+
+    def own_near(x, slot):
+        for chunk, (first, fields) in enumerate(chunks_of(x)):
+            for f in range(first, first + fields):
+                low, high = [y_ref[x, c_rows(f, half), :] for half in range(2)]
+                own_ref[slot, f, 0] = take(low, index_ref[0, 0])
+                own_ref[slot, f, 1] = take(high, index_ref[0, 0])
+                own_ref[slot, f, 2] = take(crossed(low, high), index_ref[1, 0])
+            minus = packed_rows([y_ref[x, rows, :] for rows in chunk_rows(x, chunk)], NODE1 - 1)
+            own_z[slot, chunk] = take(minus, index_ref[2, 0])
+
+    own_near(0, 0)
+    to_k_order(uc, uk)
+    volume(uc, uk, lc, tk, 1.0)
     pl.semaphore_wait(barrier, len(others))
     for chunk in range(len(CHUNKS)):
         send(0, chunk)
-    for r in range(FACE // 2, FACE):
-        transposed(0, r)
-    for f in range(1, FIELDS):
+    out_row = lax.broadcasted_iota(jnp.int32, eye_ref.shape, 0)
+    out_lane = lax.broadcasted_iota(jnp.int32, eye_ref.shape, 1)
+    eye_ref[...] = jnp.where(out_row == out_lane % LANES, 1.0, 0.0).astype(jnp.bfloat16)
+    for f in range(FIELDS):
         loaded(f)
-        for r in range(FACE):
+        for r in range(SPLIT_AT, FACE, 2):
+            transposed_pair(f, r)
+        for r in range(SPLIT_AT):
             transposed(f, r)
-    to_k_order(uc, uk)
-    volume(uc, uk, lc, tk, 1.0)
-
-    def picked(kind, values):
-        index = index_ref[kind, 0]
-        code = index_ref[kind, 1]
-        out = take(values[0], index)
-        for at_code, value in enumerate(values[1:]):
-            out = jnp.where(code == at_code + 1, take(value, index), out)
-        return out
-
-    def near_compact(x, chunk):
-        first, fields = CHUNKS[chunk]
+
+    def near_compact(x, slot, chunk):
+        first, fields = chunks_of(x)[chunk]
         sides = []
         for f in range(first, first + fields):
             low, high = [
-                [y_ref[x, c_rows(f, half), :]]
-                + [recv_ref[x, which, c_rows(f, half), :] for which in range(2)]
-                for half in range(2)
+                [recv_ref[x, which, c_rows(f, half), :] for which in range(2)] for half in range(2)
             ]
-            y = picked(1, [pltpu.roll(jnp.where(top, a, b), NODE1, 0) for a, b in zip(low, high)])
-            sides.append((picked(0, low), picked(0, high), y))
-        there = chunk_rows(chunk)
-        minus = [packed_rows([y_ref[x, rows, :] for rows in there], NODE1 - 1)]
-        for which in range(2):
-            minus.append(packed_rows([recv_ref[x, which, rows, :] for rows in there], NODE1 - 1))
+            own = [own_ref[slot, f, each] for each in range(3)]
+            y = picked(1, own[2], [crossed(a, b) for a, b in zip(low, high)])
+            sides.append((picked(0, own[0], low), picked(0, own[1], high), y))
+        there = chunk_rows(x, chunk)
+        minus = [
+            packed_rows([recv_ref[x, which, rows, :] for rows in there], NODE1 - 1) for which in range(2)
+        ]
         plus = [zrecv_ref[x, which, chunk * SUB : (chunk + 1) * SUB, :] for which in range(2)]
-        return sides, picked(2, minus), picked(3, plus)
+        plus = picked(3, take(plus[0], index_ref[3, 0]), plus[1:])
+        return sides, picked(2, own_z[slot, chunk], minus), plus
 
     def spread(value):
         turned = [value] + [pltpu.roll(value, i * count, 1) for i in range(1, NODE1)]
@@ -443,10 +480,10 @@
             plus = pltpu.roll(plus, NODE1 - 1 - slot, 0)
         return jnp.where(k_of == 0, minus, jnp.where(k_of == NODE1 - 1, plus, 0.0))
 
-    def spread_near(chunk, near, put):
+    def spread_near(x, chunk, near, put):
         sides, minus, plus = near
         minus, plus = spread(minus), spread(plus)
-        first, fields = CHUNKS[chunk]
+        first, fields = chunks_of(x)[chunk]
         for each, (x_low, x_high, y) in enumerate(sides):
             f = first + each
             for half, value in enumerate((x_low, x_high)):
@@ -461,9 +498,9 @@
 
     x_side = (group == 0) | (group == NODE1 - 1)
 
-    def lift(chunk, near, v, scale=None):
+    def lift(x, chunk, near, v, scale=None):
         sides, minus, plus = near
-        first, fields = CHUNKS[chunk]
+        first, fields = chunks_of(x)[chunk]
         for each, (x_low, x_high, y) in enumerate(sides):
             for half, value in enumerate((x_low, x_high)):
                 value = jnp.where(x_side, value, 0.0) + z_state(minus, plus, 2 * each + half)
@@ -506,7 +543,7 @@
     blocks = FIELDS * FACE // SUB
 
     def whole(xs, dst, sends):
-        for chunk, (first, fields) in enumerate(CHUNKS):
+        for chunk, (first, fields) in enumerate(chunks_of(sends[0])):
             @pl.loop(2 * first, 2 * (first + fields))
             def _(t):
                 product(t, xs, dst, (0, FIELDS), True, True)
@@ -514,18 +551,20 @@
             for x in sends:
                 send(x, chunk)
 
-    def by_chunk(xs, dst, sends, await_chunk, ready):
+    def by_chunk(source, xs, dst, sends, await_chunk, ready):
         await_chunk(0)
         ready(0)
-        for chunk, fields in enumerate(CHUNKS[:-1]):
+        arriving = chunks_of(source)
+        for chunk, fields in enumerate(arriving[:-1]):
             await_chunk(chunk + 1)
             ready(chunk + 1)
             for t in range(blocks):
                 product(t, xs, dst, fields, chunk == 0, False)
-        for chunk, (first, fields) in enumerate(CHUNKS):
+        for chunk, (first, fields) in enumerate(chunks_of(sends[0]) if sends else [(0, FIELDS)]):
             @pl.loop(2 * first, 2 * (first + fields))
             def _(t):
-                product(t, xs, dst, CHUNKS[-1], False, True)
+                product(t, xs, dst, arriving[-1], False, True)
+
             for x in sends:
                 send(x, chunk)
 
@@ -535,13 +574,14 @@
     every = range(len(CHUNKS))
     arrived([0], every)
     for chunk in every:
-        spread_near(chunk, near_compact(0, chunk), put_first)
+        spread_near(0, chunk, near_compact(0, 0, chunk), put_first)
     surface(uc, near_ref, lc, 1.0)
     whole([lc], [y_ref.at[1]], [1])
+    own_near(1, 0)
 
     def ready_v(chunk):
-        near = near_compact(1, chunk)
-        lift(chunk, near, 0)
+        near = near_compact(1, 0, chunk)
+        lift(1, chunk, near, 0)
         sides, minus, plus = near
         for each, side in enumerate(sides):
             for slot, value in enumerate(side):
@@ -549,7 +589,8 @@
         near_z[chunk, 0] = minus
         near_z[chunk, 1] = plus
 
-    by_chunk([x_ref.at[0]], [y_ref.at[2]], [2], lambda chunk: arrived([1], [chunk]), ready_v)
+    by_chunk(1, [x_ref.at[0]], [y_ref.at[2]], [2], lambda chunk: arrived([1], [chunk]), ready_v)
+    own_near(2, 0)
 
     def alpha(i):
         return time_step * sum(butcher[i])
@@ -594,7 +635,7 @@
 
     for chunk, (first, fields) in enumerate(CHUNKS):
         sides = [[near_v[f, slot] for slot in range(3)] for f in range(first, first + fields)]
-        spread_near(chunk, (sides, near_z[chunk, 0], near_z[chunk, 1]), add_v)
+        spread_near(1, chunk, (sides, near_z[chunk, 0], near_z[chunk, 1]), add_v)
     sections = range(own_sections)
     own_alphas = [per_part(lambda p, s=s: alpha(own(p, s))) for s in sections]
     own_betas = [per_part(lambda p, s=s: alpha(own(p, s)) * coupling(own(p, s))) for s in sections]
@@ -605,9 +646,9 @@
     ]
     for s in sections:
         x_ref[s] = -(own_alphas[s] * vc[...] + own_betas[s] * wc[...])
-    arrived([2], every)
     for chunk in every:
-        spread_near(chunk, near_compact(2, chunk), add_w)
+        arrived([2], [chunk])
+        spread_near(2, chunk, near_compact(2, 0, chunk), add_w)
     surface(gc, near_ref, lc, time_step)
 
     for start in range(0, unknowns, SUB):
@@ -628,9 +669,11 @@
 
     def ready_first(chunk):
         for s in sections:
-            lift(chunk, near_compact(3 + s, chunk), s, own_couplings[s])
-
-    by_chunk(operands, [last_ref.at[s] for s in sections], [], await_first, ready_first)
+            lift(3 + s, chunk, near_compact(3 + s, s, chunk), s, own_couplings[s])
+
+    for s in sections:
+        own_near(3 + s, s)
+    by_chunk(3, operands, [last_ref.at[s] for s in sections], [], await_first, ready_first)
 
     for f in range(FIELDS):
         for half in range(2):
@@ -649,7 +692,8 @@
     rows = gc[...].T
     for s in sections:
         out_ref[s] = rows[s * count : (s + 1) * count]
-    for which, there in enumerate((recv_ref, zrecv_ref)):
+    sent = sum(len(chunks_of(x)) for x in range(3 + own_sections)) * 2 * SUB
+    for which, there in enumerate((recv_ref, tt_ref.at[0, pl.ds(0, sent)])):
         pltpu.make_async_copy(there, there, send_sem.at[which]).wait()
 
 
@@ -661,7 +705,7 @@
     exchanges = 3 + own_sections
     column = pltpu.VMEM((unknowns, LANES), jnp.float32)
     compact = FIELDS * FACE
-    packed = len(CHUNKS) * SUB
+    packed = len(FINE) * SUB
     change = pl.pallas_call(
         functools.partial(kernel, devices, count),
         out_shape=pltpu.VMEM((own_sections, count, unknowns), jnp.float32),
@@ -681,16 +725,19 @@
             pltpu.VMEM((FIELDS, 3, SUB, LANES), jnp.float32),
             pltpu.VMEM((len(CHUNKS), 2, SUB, LANES), jnp.float32),
             pltpu.VMEM((16, FIELDS, SUB, LANES), jnp.float32),
+            pltpu.VMEM((own_sections, FIELDS, 3, SUB, LANES), jnp.float32),
+            pltpu.VMEM((own_sections, len(FINE), SUB, LANES), jnp.float32),
         ]
         + [column] * 7
         + [
             pltpu.VMEM((own_sections, unknowns, LANES), jnp.float32),
             pltpu.VMEM((own_sections, compact // SUB, SUB, SUB, LANES), jnp.float32),
             pltpu.VMEM((own_sections, compact, LANES), jnp.float32),
+            pltpu.VMEM((LANES, 2 * LANES), jnp.bfloat16),
             pltpu.SemaphoreType.DMA((3,)),
             pltpu.SemaphoreType.DMA((len(LOADS),)),
             pltpu.SemaphoreType.DMA((2,)),
-            pltpu.SemaphoreType.DMA((8,)),
+            pltpu.SemaphoreType.DMA((1 + 2 * len(CHUNKS) + len(FINE),)),
         ],
         compiler_params=pltpu.CompilerParams(
             collective_id=0, has_side_effects=True, vmem_limit_bytes=VMEM_BYTES

time: 29.9 us -> 28.7 us (0.960)
  Pallas kernels: 29.1 us -> 27.9 us
    pallas_call x1, Pallas kernels: 29.1 us -> 27.9 us  [on_device(): pl.pallas_call(functools.partial(kernel, devices, count), out_shape=pltpu...]
where the time goes in v4:
time: 28.7 us; the launch traced here: 28.5 us
  Pallas kernels  27.9 us (97%)
  other arithmetic  0.65 us (2%)
    pallas_call x1, Pallas kernels, on_device(): pl.pallas_call(functools.partial(kernel, devices, count), out_shape=pltpu...  27.9 us
    add x1, other arithmetic, on_device(): return u_start[None] + change  0.65 us

profile of v4, /device:TPU:0, one launch (start us, length us, event | category | flops | bytes accessed | tf_op | source)
XLA Modules:
  0.0 28.5 jit_solution(13955144017760726659)
XLA Ops:
  0.0 0.0 copy-start
  0.0 27.9 %shard_map.46 = f32[2,32,320]{2,1,0:T(8,128)S(1)} custom-call(f32[32,320]{1,0:T(8,128)} %u_in.1, s32[5,32]{1,0:T(8,128)} %bitcast.2, s32[4,128]{1,0:T(4,128)} %bitcast.3, f32[32,320,320]{2,1,0:T(8,128)} %inv_ref.1), custom_call_target="tpu_custom_call" | custom-call | tf_op jit(solution)/shard_map/pallas_call | solution.py:709
  27.9 0.0 copy-done
  27.9 0.7 %broadcast_add_fusion = f32[2,32,320]{2,1,0:T(8,128)} fusion(f32[2,32,320]{2,1,0:T(8,128)S(1)} %shard_map.46, f32[32,320]{1,0:T(8,128)S(1)} %copy-done), kind=kLoop, calls=%fused_computation | loop fusion | flops 20480 | bytes 204800 | tf_op jit(solution)/shard_map/add | solution.py:746
Async XLA Ops:
  0.0 27.9 %copy-start = (f32[32,320]{1,0:T(8,128)S(1)}, f32[32,320]{1,0:T(8,128)}, u32[]{:S(2)}) copy-start(f32[32,320]{1,0:T(8,128)} %u_in.1) | copy-start | bytes 122884

commit v5 on v4

--- a/solution.py
+++ b/solution.py
@@ -222,7 +222,7 @@
 
 
 def chunks_of(x):
-    return FINE if x > 2 else CHUNKS
+    return CHUNKS if x in (0, 2) else FINE
 
 
 def near_state(near_ref, slot):
@@ -252,10 +252,12 @@
     def at(offset):
         return lax.rem(rank + (offset + devices), devices)
 
-    barrier = pltpu.get_barrier_semaphore()
-    others = (1, -1, rotation, -rotation, rotation + 1, -rotation - 1)
-    for offset in others:
-        pl.semaphore_signal(barrier, inc=1, device_id={"elem": at(offset)}, device_id_type=MESH)
+    def load(part_of):
+        first, fields = LOADS[part_of]
+        rows = pl.ds(first * NODES, fields * NODES)
+        for e in range(count):
+            pltpu.make_async_copy(inv_ref.at[e, rows], raw_ref.at[rows, e], a_sem.at[part_of]).start()
+
     small = [
         pltpu.make_async_copy(src, dst, in_sem.at[index])
         for index, (src, dst) in enumerate(
@@ -264,13 +266,10 @@
     ]
     for each in small:
         each.start()
-
-    def load(part_of):
-        first, fields = LOADS[part_of]
-        rows = pl.ds(first * NODES, fields * NODES)
-        for e in range(count):
-            pltpu.make_async_copy(inv_ref.at[e, rows], raw_ref.at[rows, e], a_sem.at[part_of]).start()
-
+    barrier = pltpu.get_barrier_semaphore()
+    others = (1, -1, rotation, -rotation, rotation + 1, -rotation - 1)
+    for offset in others:
+        pl.semaphore_signal(barrier, inc=1, device_id={"elem": at(offset)}, device_id_type=MESH)
     def loaded(part_of):
         first, fields = LOADS[part_of]
         there = raw_ref.at[pl.ds(first * NODES, fields * NODES)]
@@ -303,8 +302,8 @@
             for each in range(2):
                 tt_ref[f * FACE + r + each, q : q + width, :] = out[:, each * LANES : (each + 1) * LANES]
 
-    load(0)
-    load(1)
+    for part_of in range(len(LOADS)):
+        load(part_of)
 
     row = lax.broadcasted_iota(jnp.int32, (SUB, LANES), 0)
     lane = lax.broadcasted_iota(jnp.int32, (SUB, LANES), 1)
@@ -317,7 +316,7 @@
     def event(x, chunk):
         if x == 0:
             return 0
-        return 1 + chunk + (min(x, 3) - 1) * len(CHUNKS)
+        return 1 + chunk + sum(len(chunks_of(each)) for each in range(1, min(x, 3)))
 
     def copies(x, chunk):
         first, fields = chunks_of(x)[chunk]
@@ -371,8 +370,11 @@
                 value = jnp.where(group == i, uc[g_rows(f, i, half), :], value)
             y_ref[0, c_rows(f, half), :] = value
 
-    for part_of in range(2, len(LOADS)):
-        load(part_of)
+    to_k_order(uc, uk)
+    volume(uc, uk, lc, tk, 1.0)
+    pl.semaphore_wait(barrier, len(others))
+    for chunk in range(len(CHUNKS)):
+        send(0, chunk)
 
     def found(wanted, offsets):
         index = wanted - at(offsets[0]) * count
@@ -430,11 +432,6 @@
             own_z[slot, chunk] = take(minus, index_ref[2, 0])
 
     own_near(0, 0)
-    to_k_order(uc, uk)
-    volume(uc, uk, lc, tk, 1.0)
-    pl.semaphore_wait(barrier, len(others))
-    for chunk in range(len(CHUNKS)):
-        send(0, chunk)
     out_row = lax.broadcasted_iota(jnp.int32, eye_ref.shape, 0)
     out_lane = lax.broadcasted_iota(jnp.int32, eye_ref.shape, 1)
     eye_ref[...] = jnp.where(out_row == out_lane % LANES, 1.0, 0.0).astype(jnp.bfloat16)
@@ -535,7 +532,7 @@
                     accs[v][a] = term if accs[v][a] is None else accs[v][a] + term
         for v in range(vectors):
             if last:
-                dst[v][pl.ds(pl.multiple_of(t * SUB, SUB), SUB), :] = folded(accs[v])
+                dst[v][t * SUB : (t + 1) * SUB, :] = folded(accs[v])
             else:
                 for a in range(SUB):
                     acc_ref[v, t, a] = accs[v][a]
@@ -544,10 +541,8 @@
 
     def whole(xs, dst, sends):
         for chunk, (first, fields) in enumerate(chunks_of(sends[0])):
-            @pl.loop(2 * first, 2 * (first + fields))
-            def _(t):
+            for t in range(2 * first, 2 * (first + fields)):
                 product(t, xs, dst, (0, FIELDS), True, True)
-
             for x in sends:
                 send(x, chunk)
 
@@ -561,10 +556,8 @@
             for t in range(blocks):
                 product(t, xs, dst, fields, chunk == 0, False)
         for chunk, (first, fields) in enumerate(chunks_of(sends[0]) if sends else [(0, FIELDS)]):
-            @pl.loop(2 * first, 2 * (first + fields))
-            def _(t):
+            for t in range(2 * first, 2 * (first + fields)):
                 product(t, xs, dst, arriving[-1], False, True)
-
             for x in sends:
                 send(x, chunk)
 
@@ -585,7 +578,7 @@
         sides, minus, plus = near
         for each, side in enumerate(sides):
             for slot, value in enumerate(side):
-                near_v[CHUNKS[chunk][0] + each, slot] = value
+                near_v[chunks_of(1)[chunk][0] + each, slot] = value
         near_z[chunk, 0] = minus
         near_z[chunk, 1] = plus
 
@@ -633,7 +626,7 @@
     def add_w(slot, f, value):
         near_ref[slot, f] = near_ref[slot, f] + betas * value
 
-    for chunk, (first, fields) in enumerate(CHUNKS):
+    for chunk, (first, fields) in enumerate(chunks_of(1)):
         sides = [[near_v[f, slot] for slot in range(3)] for f in range(first, first + fields)]
         spread_near(1, chunk, (sides, near_z[chunk, 0], near_z[chunk, 1]), add_v)
     sections = range(own_sections)
@@ -693,7 +686,7 @@
     for s in sections:
         out_ref[s] = rows[s * count : (s + 1) * count]
     sent = sum(len(chunks_of(x)) for x in range(3 + own_sections)) * 2 * SUB
-    for which, there in enumerate((recv_ref, tt_ref.at[0, pl.ds(0, sent)])):
+    for which, there in enumerate((recv_ref, tt_ref.at[pl.ds(0, 2), pl.ds(0, sent // 2)])):
         pltpu.make_async_copy(there, there, send_sem.at[which]).wait()
 
 
@@ -723,7 +716,7 @@
             pltpu.VMEM((exchanges, 2, packed, LANES), jnp.float32),
             pltpu.VMEM((4, 2, SUB, LANES), jnp.int32),
             pltpu.VMEM((FIELDS, 3, SUB, LANES), jnp.float32),
-            pltpu.VMEM((len(CHUNKS), 2, SUB, LANES), jnp.float32),
+            pltpu.VMEM((len(FINE), 2, SUB, LANES), jnp.float32),
             pltpu.VMEM((16, FIELDS, SUB, LANES), jnp.float32),
             pltpu.VMEM((own_sections, FIELDS, 3, SUB, LANES), jnp.float32),
             pltpu.VMEM((own_sections, len(FINE), SUB, LANES), jnp.float32),
@@ -737,7 +730,7 @@
             pltpu.SemaphoreType.DMA((3,)),
             pltpu.SemaphoreType.DMA((len(LOADS),)),
             pltpu.SemaphoreType.DMA((2,)),
-            pltpu.SemaphoreType.DMA((1 + 2 * len(CHUNKS) + len(FINE),)),
+            pltpu.SemaphoreType.DMA((1 + len(CHUNKS) + 2 * len(FINE),)),
         ],
         compiler_params=pltpu.CompilerParams(
             collective_id=0, has_side_effects=True, vmem_limit_bytes=VMEM_BYTES

time: 28.7 us -> 27.9 us (0.972)
  Pallas kernels: 27.9 us -> 27.1 us
    pallas_call x1, Pallas kernels: 27.9 us -> 27.1 us  [on_device(): pl.pallas_call(functools.partial(kernel, devices, count), out_shape=pltpu...]
where the time goes in v5:
time: 27.9 us; the launch traced here: 27.8 us
  Pallas kernels  27.1 us (97%)
  other arithmetic  0.65 us (2%)
    pallas_call x1, Pallas kernels, on_device(): pl.pallas_call(functools.partial(kernel, devices, count), out_shape=pltpu...  27.1 us
    add x1, other arithmetic, on_device(): return u_start[None] + change  0.65 us

profile of v5, /device:TPU:0, one launch (start us, length us, event | category | flops | bytes accessed | tf_op | source)
XLA Modules:
  0.0 27.8 jit_solution(4034134472293982056)
XLA Ops:
  0.0 0.0 copy-start
  0.0 27.1 %shard_map.46 = f32[2,32,320]{2,1,0:T(8,128)S(1)} custom-call(f32[32,320]{1,0:T(8,128)} %u_in.1, s32[5,32]{1,0:T(8,128)} %bitcast.2, s32[4,128]{1,0:T(4,128)} %bitcast.3, f32[32,320,320]{2,1,0:T(8,128)} %inv_ref.1), custom_call_target="tpu_custom_call" | custom-call | tf_op jit(solution)/shard_map/pallas_call | solution.py:702
  27.1 0.0 copy-done
  27.1 0.7 %broadcast_add_fusion = f32[2,32,320]{2,1,0:T(8,128)} fusion(f32[2,32,320]{2,1,0:T(8,128)S(1)} %shard_map.46, f32[32,320]{1,0:T(8,128)S(1)} %copy-done), kind=kLoop, calls=%fused_computation | loop fusion | flops 20480 | bytes 204800 | tf_op jit(solution)/shard_map/add | solution.py:739
Async XLA Ops:
  0.0 27.1 %copy-start = (f32[32,320]{1,0:T(8,128)S(1)}, f32[32,320]{1,0:T(8,128)}, u32[]{:S(2)}) copy-start(f32[32,320]{1,0:T(8,128)} %u_in.1) | copy-start | bytes 122884

commit v6 on v5

--- a/solution.py
+++ b/solution.py
@@ -546,20 +546,26 @@
             for x in sends:
                 send(x, chunk)
 
-    def by_chunk(source, xs, dst, sends, await_chunk, ready):
+    def by_chunk(source, xs, dst, sends, await_chunk, ready, finish=None, lead=0):
         await_chunk(0)
         ready(0)
         arriving = chunks_of(source)
         for chunk, fields in enumerate(arriving[:-1]):
-            await_chunk(chunk + 1)
-            ready(chunk + 1)
+            if chunk >= lead:
+                await_chunk(chunk + 1)
+                ready(chunk + 1)
             for t in range(blocks):
                 product(t, xs, dst, fields, chunk == 0, False)
-        for chunk, (first, fields) in enumerate(chunks_of(sends[0]) if sends else [(0, FIELDS)]):
+            if chunk < lead:
+                await_chunk(chunk + 1)
+                ready(chunk + 1)
+        for chunk, (first, fields) in enumerate(chunks_of(sends[0]) if sends else FINE):
             for t in range(2 * first, 2 * (first + fields)):
                 product(t, xs, dst, arriving[-1], False, True)
             for x in sends:
                 send(x, chunk)
+            if finish is not None:
+                finish(chunk)
 
     def put_first(slot, f, value):
         near_ref[slot, f] = value
@@ -666,25 +672,39 @@
 
     for s in sections:
         own_near(3 + s, s)
-    by_chunk(3, operands, [last_ref.at[s] for s in sections], [], await_first, ready_first)
+    def kept(f, half, s):
+        start = ((2 * s + half) * FIELDS + f) * SUB
+        return slice(start, start + SUB)
 
     for f in range(FIELDS):
         for half in range(2):
             rows = c_rows(f, half)
+            for s in sections:
+                vc[kept(f, half, s), :] = (
+                    own_alphas[s] * y_ref[1, rows, :]
+                    + own_betas[s] * y_ref[2, rows, :]
+                    + y_ref[3 + s, rows, :]
+                )
+
+    def finish(f):
+        for half in range(2):
             values = [
-                own_alphas[s] * y_ref[1, rows, :] + own_betas[s] * y_ref[2, rows, :]
-                + y_ref[3 + s, rows, :] + last_ref[s, rows, :]
-                for s in sections
+                spread(vc[kept(f, half, s), :] + last_ref[s, c_rows(f, half), :]) for s in sections
             ]
-            values = [spread(value) for value in values]
             for i in range(NODE1):
                 value = values[0][i]
                 for s in sections[1:]:
                     value = jnp.where(group == s, values[s][i], value)
                 gc[g_rows(f, i, half), :] = value
-    rows = gc[...].T
-    for s in sections:
-        out_ref[s] = rows[s * count : (s + 1) * count]
+        if f % 2 or f == FIELDS - 1:
+            first = f - f % 2
+            columns = slice(first * NODES, (f + 1) * NODES)
+            done = gc[columns, :].T
+            for s in sections:
+                out_ref[s, :, columns] = done[s * count : (s + 1) * count]
+
+    by_chunk(3, operands, [last_ref.at[s] for s in sections], [], await_first, ready_first, finish, 2)
+
     sent = sum(len(chunks_of(x)) for x in range(3 + own_sections)) * 2 * SUB
     for which, there in enumerate((recv_ref, tt_ref.at[pl.ds(0, 2), pl.ds(0, sent // 2)])):
         pltpu.make_async_copy(there, there, send_sem.at[which]).wait()

time: 27.9 us -> 27.8 us (level)
  no operation moved by 1% of the time
where the time goes in v6:
time: 27.8 us; the launch traced here: 27.7 us
  Pallas kernels  27 us (97%)
  other arithmetic  0.65 us (2%)
    pallas_call x1, Pallas kernels, on_device(): pl.pallas_call(functools.partial(kernel, devices, count), out_shape=pltpu...  27 us
    add x1, other arithmetic, on_device(): return u_start[None] + change  0.65 us

profile of v6, /device:TPU:0, one launch (start us, length us, event | category | flops | bytes accessed | tf_op | source)
XLA Modules:
  0.0 27.7 jit_solution(4644570321424089550)
XLA Ops:
  0.0 0.0 copy-start
  0.0 27.0 %shard_map.46 = f32[2,32,320]{2,1,0:T(8,128)S(1)} custom-call(f32[32,320]{1,0:T(8,128)} %u_in.1, s32[5,32]{1,0:T(8,128)} %bitcast.2, s32[4,128]{1,0:T(4,128)} %bitcast.3, f32[32,320,320]{2,1,0:T(8,128)} %inv_ref.1), custom_call_target="tpu_custom_call" | custom-call | tf_op jit(solution)/shard_map/pallas_call | solution.py:722
  27.0 0.0 copy-done
  27.0 0.7 %broadcast_add_fusion = f32[2,32,320]{2,1,0:T(8,128)} fusion(f32[2,32,320]{2,1,0:T(8,128)S(1)} %shard_map.46, f32[32,320]{1,0:T(8,128)S(1)} %copy-done), kind=kLoop, calls=%fused_computation | loop fusion | flops 20480 | bytes 204800 | tf_op jit(solution)/shard_map/add | solution.py:759
Async XLA Ops:
  0.0 27.0 %copy-start = (f32[32,320]{1,0:T(8,128)S(1)}, f32[32,320]{1,0:T(8,128)}, u32[]{:S(2)}) copy-start(f32[32,320]{1,0:T(8,128)} %u_in.1) | copy-start | bytes 122884
